TPU v7x, 512 devices: a whole 4x4x16 slice. The times are simulated.
512 devices in a mesh: req: 64 (over z, x), head: 8 (over y, core).
Axes of the slice: x: 4, y: 4, z: 16, core: 2. Of those that a mesh axis runs over, the one named last changes fastest.
Arguments:
- tokens: bfloat16 [64, 512, 1024], P('req', 'head'), may hold values from -6 to 6
- gain: bfloat16 [1024], replicated, may hold values from 0.099609375 to 1.8984375
- projection_weight: bfloat16 [1024, 4, 1024], P(None, None, 'head'), may hold values from -0.1875 to 0.1875
- output_weight: bfloat16 [1024, 1024], P('head'), may hold values from -0.1875 to 0.1875
- persist: bfloat16 [2, 16, 1024], P(None, None, 'head'), may hold values from -6 to 6
- cache_page_slots: bfloat16 [64, 64, 64, 2, 1024], P('req', None, None, None, 'head'), may hold values from -250 to 250
- cached_length: int32 [64], P('req'), may hold values from 33 to 4096, as said below
- page_keeper: int32 [64, 128], P('req'), may hold values from -1 to 63, as said below
- page_slot_index: int32 [64, 128], P('req'), may hold values from -1 to 1, as said below
- memory_state: float32 [2, 64, 8, 128, 128], P(None, 'req', 'head'), may hold values from -3 to 3
- retention: float32 [64, 8], P('req', 'head'), may hold values from 0.2 to 1
- momentum: float32 [64, 8], P('req', 'head'), may hold values from 0.2 to 0.9
- memory_step_scale: float32 [64, 8], P('req', 'head'), may hold values from 0.02 to 0.3
- halving_updates: int32 [64, 8], P('req'), may hold values 0 or 1
Outputs:
- layer_out: bfloat16 [64, 512, 1024], P('req', 'head')
- new_state: float32 [2, 64, 8, 128, 128], P(None, 'req', 'head')
Inputs may be any that keep to these rules, and one draw needn't show every extreme that they name: `cached_length`: the requests of one device hold together at most 128 pages. `page_keeper`: pages j below cached_length[r] / 32 (rounded up) have a keeper; later entries are -1. No keeper and slot serve two pages of the requests of one device. `page_slot_index`: -1 exactly where page_keeper is -1.
All inputs are finite; a program needn't handle non-finite values. No bound on the sum of `halving_updates` on one device may be relied on, other than what follows from the above.
Results may differ from a plain program's by a relative error of at most 0.012.
The roundings to bfloat16 on the way count: a program that leaves them out, or rounds other values in their place, can miss the bound.
Values may be sent and summed in bfloat16 or wider, within the bound.
A program may use at most 64 MiB of HBM per device.

v0:
```python
import math

import jax
import jax.numpy as jnp
from jax import lax
from jax.sharding import PartitionSpec as P

HD = 128
BLK = 64
PAGE = 32


norm_eps = 1e-05
unit_eps = 1e-06


def unit_rows(values_f):
    return values_f * lax.rsqrt(jnp.sum(values_f * values_f, axis=-1, keepdims=True) + unit_eps)


def against(left, right):
    return lax.dot_general(
        left, right, (((1,), (1,)), ((), ())), preferred_element_type=jnp.float32
    )


def exact_rows(left, right):
    return lax.dot_general(
        left,
        right,
        (((1,), (1,)), ((), ())),
        precision=lax.Precision.HIGHEST,
        preferred_element_type=jnp.float32,
    )


def exact_outer(left, right):
    return lax.dot_general(
        left,
        right,
        (((0,), (0,)), ((), ())),
        precision=lax.Precision.HIGHEST,
        preferred_element_type=jnp.float32,
    )


def shards(
    tokens,
    gain,
    projection_weight,
    output_weight,
    persist,
    cache_page_slots,
    cached_length,
    page_keeper,
    page_slot_index,
    memory_state,
    retention,
    momentum,
    memory_step_scale,
    halving_updates,
):
    req_dev = tokens.shape[0]
    width = tokens.shape[2]
    head_cols = projection_weight.shape[2]
    homes = cache_page_slots.shape[1]
    lanes = cache_page_slots.shape[2] // PAGE
    max_pages = page_keeper.shape[1]
    scale = 1.0 / math.sqrt(HD)
    gain_f = gain.astype(jnp.float32)
    flat_w = projection_weight.reshape(width, 4 * head_cols)
    piece_f = lax.all_gather(tokens, "head", axis=1, tiled=True).astype(jnp.float32)
    scaled = (
        piece_f * lax.rsqrt(jnp.mean(piece_f * piece_f, axis=-1, keepdims=True) + norm_eps) * gain_f
    )
    normed = scaled.astype(jnp.bfloat16)
    count = normed.shape[0] * normed.shape[1]
    result = jnp.dot(normed.reshape(count, width), flat_w, preferred_element_type=jnp.float32)
    projected = result.reshape(normed.shape[0], normed.shape[1], 4, head_cols)
    queries = projected[:, :, 0].astype(jnp.bfloat16)
    own_keys = projected[:, :, 1].astype(jnp.bfloat16)
    own_values = projected[:, :, 2].astype(jnp.bfloat16)
    gates = projected[:, :, 3]
    prefill = queries.shape[1]
    kept_span = lanes * PAGE
    received = lax.all_to_all(cache_page_slots, "req", split_axis=1, concat_axis=0, tiled=True)
    cache_keys = received[:, 0, :, 0, :].reshape(homes * kept_span, head_cols)
    cache_values = received[:, 0, :, 1, :].reshape(homes * kept_span, head_cols)
    page_ids = jnp.arange(max_pages, dtype=jnp.int32)
    filled = jnp.clip(cached_length[:, None] - page_ids[None, :] * PAGE, 0, PAGE)
    slot_of = page_keeper * lanes + page_slot_index
    slot_ids = jnp.arange(homes * lanes, dtype=jnp.int32)
    slot_fill = jnp.sum(
        jnp.where(slot_of[:, :, None] == slot_ids[None, None, :], filled[:, :, None], 0), axis=1
    )
    position = jnp.arange(PAGE, dtype=jnp.int32)
    full_valid = (position[None, None, :] < slot_fill[:, :, None]).reshape(
        req_dev, homes, lanes * PAGE
    )
    cache_valid = full_valid.reshape(req_dev, homes * kept_span)
    causal = jnp.arange(prefill)[:, None] >= jnp.arange(prefill)[None, :]
    upper_col = HD
    query_head = queries[0, :, 0:upper_col]
    key_head = own_keys[0, :, 0:upper_col]
    value_head = own_values[0, :, 0:upper_col]
    score_p = against(query_head, persist[0, :, 0:upper_col]) * scale
    score_c = jnp.where(cache_valid[0][None, :], against(query_head, cache_keys) * scale, -jnp.inf)
    score_t = jnp.where(causal, against(query_head, key_head) * scale, -jnp.inf)
    row_max = jnp.maximum(
        jnp.maximum(
            jnp.max(score_p, axis=-1, keepdims=True), jnp.max(score_c, axis=-1, keepdims=True)
        ),
        jnp.max(score_t, axis=-1, keepdims=True),
    )
    exp_p = jnp.exp(score_p - row_max)
    exp_c = jnp.exp(score_c - row_max)
    exp_t = jnp.exp(score_t - row_max)
    total = (
        jnp.sum(exp_p, axis=-1, keepdims=True)
        + jnp.sum(exp_c, axis=-1, keepdims=True)
        + jnp.sum(exp_t, axis=-1, keepdims=True)
    )
    mixed = jnp.dot(
        exp_p.astype(jnp.bfloat16), persist[1, :, 0:upper_col], preferred_element_type=jnp.float32
    )
    mixed = mixed + jnp.dot(
        exp_c.astype(jnp.bfloat16), cache_values, preferred_element_type=jnp.float32
    )
    mixed = mixed + jnp.dot(
        exp_t.astype(jnp.bfloat16), value_head, preferred_element_type=jnp.float32
    )
    attended = mixed / total
    unit_attn = attended * lax.rsqrt(
        jnp.mean(attended * attended, axis=-1, keepdims=True) + unit_eps
    )
    query_unit = unit_rows(query_head.astype(jnp.float32))
    key_unit = unit_rows(key_head.astype(jnp.float32))
    value_f = value_head.astype(jnp.float32)
    state_m = memory_state[0, 0, 0]
    state_s = memory_state[1, 0, 0]
    reads = []
    for block_span in range(prefill // BLK):
        lower = block_span * BLK
        q_block = query_unit[lower : lower + BLK]
        k_block = key_unit[lower : lower + BLK]
        v_block = value_f[lower : lower + BLK]
        reads.append(exact_rows(q_block, state_m))
        errors = exact_rows(k_block, state_m) - v_block
        grads = exact_outer(errors, k_block)
        state_s = momentum[0, 0] * state_s - memory_step_scale[0, 0] * grads
        keeper_list = retention[0, 0] * jnp.where(halving_updates[0, block_span] == 1, 0.5, 1.0)
        state_m = keeper_list * state_m + state_s
    memory_read = jnp.concatenate(reads, axis=0)
    head_outs = unit_attn + jax.nn.sigmoid(gates[0, :, 0:upper_col]) * memory_read
    head_states = [jnp.stack([state_m, state_s])]
    request_outs = [head_outs.astype(jnp.bfloat16)]
    state_rows = [jnp.stack(head_states, axis=1)]
    mixed_heads = jnp.stack(request_outs)
    new_state = jnp.stack(state_rows, axis=1)
    regrouped = lax.all_to_all(mixed_heads, "head", split_axis=1, concat_axis=2, tiled=True)
    row_count = regrouped.shape[1]
    piece = lax.all_gather(output_weight, "head", axis=0, tiled=True)
    groups = piece.shape[0] // head_cols
    section = regrouped
    section = section.reshape(req_dev, row_count, groups, head_cols)
    blocks = piece.reshape(groups, head_cols, width)
    sums = jnp.einsum("atgc,gcd->atgd", section, blocks, preferred_element_type=jnp.float32)
    rounded = lax.optimization_barrier(sums.astype(jnp.bfloat16))
    layer_f = jnp.sum(rounded.astype(jnp.float32), axis=2)
    return (layer_f.astype(jnp.bfloat16), new_state)


def solution(mesh):
    in_specs = (
        P("req", "head", None),
        P(),
        P(None, None, "head"),
        P("head", None),
        P(None, None, "head"),
        P("req", None, None, None, "head"),
        P("req"),
        P("req", None),
        P("req", None),
        P(None, "req", "head", None, None),
        P("req", "head"),
        P("req", "head"),
        P("req", "head"),
        P("req", None),
    )
    out_specs = (P("req", "head", None), P(None, "req", "head", None, None))
    return jax.shard_map(shards, mesh=mesh, in_specs=in_specs, out_specs=out_specs, check_vma=False)
```

profile of v0, /device:TPU:1, one launch (start us, length us, event | category | flops | bytes accessed | tf_op | source)
XLA Modules:
  0.0 161.1 jit_solution(271079519594700890)
XLA Ops:
  7.3 0.7 all-gather.3.cloned.1.call-update
  7.9 3.5 %copy.44 = bf16[1,64,64,2,128]{4,2,3,0,1:T(8,128)(2,1)} copy(bf16[1,64,64,2,128]{4,3,2,1,0:T(2,128)(2,1)} %param.19) | data formatting | bytes 4194304 | tf_op args[5]
  11.4 19.2 %all-to-all-start = ((bf16[1,64,64,2,128]{4,2,3,0,1:T(8,128)(2,1)}), bf16[1,64,64,2,128]{4,2,3,0,1:T(8,128)(2,1)S(1)}, u32[]{:S(2)}, u32[]{:S(2)}) async-start(bf16[1,64,64,2,128]{4,2,3,0,1:T(8,128)(2,1)} %copy.44), calls=%async_computation | async-start | bytes 4194304 | tf_op jit(solution)/shard_map/all_to_all | solution.py:86
  30.7 0.7 all-gather.5.cloned.1.call-update
  31.4 1.4 copy.60
  32.9 1.3 copy.43
  34.2 0.7 fusion.85
  43.0 3.8 %all-gather.3.cloned.1.call-done = bf16[1,512,1024]{2,1,0:T(8,128)(2,1)} async-done(((bf16[1,64,1024]{2,1,0:T(8,128)(2,1)}), bf16[1,512,1024]{2,1,0:T(8,128)(2,1)}) %all-gather.3.cloned.1.call-update) | async-done | bytes 1048592 | tf_op jit(solution)/shard_map/all_gather | solution.py:72
  46.8 1.5 fusion.6
  48.3 2.3 %convolution_bitcast_fusion = f32[1,512,4,128]{3,1,2,0:T(8,128)S(1)} fusion(bf16[4,128,1024]{2,1,0:T(8,128)(2,1)} %bitcast.161, bf16[1,512,1024]{2,1,0:T(8,128)(2,1)} %all-gather.3.cloned.1.call-done, f32[1024]{0:T(1024)S(1)} %convert_element_type.76, f32[512]{0:T(512)S(1)} %add_rsqrt_fusion.3), kind=kOutput, calls=%fused_computation.17 | convolution fusion | flops 538968064 | bytes 3151872 | tf_op jit(solution)/shard_map/dot_general | solution.py:78
  51.2 0.2 convolution_dynamic-update-slice_fusion.7
  51.5 0.2 convolution_subtract_fusion.7
  51.7 0.3 fusion.43
  52.0 0.2 convolution_dynamic-update-slice_fusion.6
  52.3 0.2 convolution_subtract_fusion.6
  52.5 0.3 multiply_add_fusion.5
  52.8 0.2 convolution_dynamic-update-slice_fusion.5
  53.1 0.2 convolution_subtract_fusion.5
  53.3 0.3 multiply_add_fusion.4
  53.6 0.2 convolution_dynamic-update-slice_fusion.4
  53.9 0.2 convolution_subtract_fusion.4
  54.1 0.3 multiply_add_fusion.3
  54.4 0.2 convolution_dynamic-update-slice_fusion.3
  54.7 0.2 convolution_subtract_fusion.3
  54.9 0.3 multiply_add_fusion.2
  55.2 0.2 convolution_dynamic-update-slice_fusion.2
  55.5 0.2 convolution_subtract_fusion.2
  55.7 0.3 multiply_add_fusion.1
  56.0 0.2 convolution_dynamic-update-slice_fusion.1
  56.3 0.2 convolution_subtract_fusion.1
  56.5 0.3 multiply_add_fusion
  56.8 0.2 convolution_dynamic-update-slice_fusion
  57.1 0.2 convolution_subtract_fusion
  57.5 0.3 fusion.12
  57.8 0.3 fusion.86
  58.1 67.5 %all-to-all-done = bf16[1,64,64,2,128]{4,2,3,0,1:T(8,128)(2,1)S(1)} async-done(((bf16[1,64,64,2,128]{4,2,3,0,1:T(8,128)(2,1)}), bf16[1,64,64,2,128]{4,2,3,0,1:T(8,128)(2,1)S(1)}, u32[]{:S(2)}, u32[]{:S(2)}) %all-to-all-start) | async-done | bytes 2097184 | tf_op jit(solution)/shard_map/all_to_all | solution.py:86
  126.0 1.4 fusion
  127.7 2.2 %fusion.1 = f32[512]{0:T(512)S(1)} fusion(f32[512,4096]{1,0:T(8,128)S(1)} %get-tuple-element.44, f32[512]{0:T(512)S(1)} %maximum_maximum_fusion, pred[4096]{0:T(1024)(128)(4,1)S(1)} %lt.27), kind=kLoop, calls=%fused_computation.3 | loop fusion | flops 8388096 | bytes 8396800 | tf_op jit(solution)/shard_map/reduce_sum | solution.py:120
  129.9 1.7 %fusion.3 = f32[512,128]{1,0:T(8,128)S(1)} fusion(bf16[4096,128]{1,0:T(8,128)(2,1)S(1)} %bitcast.162, f32[512,4096]{1,0:T(8,128)S(1)} %get-tuple-element.44, f32[512]{0:T(512)S(1)} %maximum_maximum_fusion, pred[4096]{0:T(1024)(128)(4,1)S(1)} %lt.27), kind=kOutput, calls=%fused_computation.5 | convolution fusion | flops 545259520 | bytes 9705472 | tf_op jit(solution)/shard_map/dot_general | solution.py:126
  131.9 0.5 multiply_reduce_fusion
  132.7 0.5 broadcast.141
  133.2 1.4 reduce.4
  134.7 0.7 reshape.270
  135.3 10.6 %all-to-all-start.1 = ((bf16[8,2,4096]{2,1,0:T(2,128)(2,1)}), bf16[8,2,4096]{2,1,0:T(2,128)(2,1)S(1)}, u32[]{:S(2)}, u32[]{:S(2)}) async-start(bf16[8,2,4096]{2,1,0:T(2,128)(2,1)} %reshape.270), calls=%async_computation.1 | async-start | bytes 262144 | tf_op jit(solution)/shard_map/all_to_all | solution.py:160
  146.0 0.7 maximum_bitcast_fusion
  146.6 4.6 %all-to-all-done.1 = bf16[8,2,4096]{2,1,0:T(2,128)(2,1)S(1)} async-done(((bf16[8,2,4096]{2,1,0:T(2,128)(2,1)}), bf16[8,2,4096]{2,1,0:T(2,128)(2,1)S(1)}, u32[]{:S(2)}, u32[]{:S(2)}) %all-to-all-start.1) | async-done | bytes 131104 | tf_op jit(solution)/shard_map/all_to_all | solution.py:160
  151.4 2.0 %fusion.9 = bf16[1,64,8,1024]{3,1,2,0:T(8,128)(2,1)S(1)} fusion(bf16[64,8,128]{2,0,1:T(8,128)(2,1)S(1)} %bitcast.164, bf16[8,128,1024]{2,1,0:T(8,128)(2,1)} %bitcast.157), kind=kOutput, calls=%fused_computation.14 | convolution fusion | flops 134742016 | bytes 3276800 | tf_op jit(solution)/shard_map/atgc,gcd->atgd/dot_general | solution.py:167
  153.4 0.8 reduce_sum.94
  (53 shorter events, 2.6 us)
Async XLA Ops:
  7.2 27.0 %copy-start.7 = (bf16[1024]{0:T(1024)(128)(2,1)S(1)}, bf16[1024]{0:T(1024)(128)(2,1)}, u32[]{:S(2)}) copy-start(bf16[1024]{0:T(1024)(128)(2,1)} %param.15) | copy-start | bytes 6148
  7.2 27.0 %copy-start.5 = (s32[1,8]{1,0:T(1,128)S(1)}, s32[1,8]{1,0:T(1,128)}, u32[]{:S(2)}) copy-start(s32[1,8]{1,0:T(1,128)} %param.27) | copy-start | bytes 100
  7.2 35.4 %copy-start.9 = (s32[1,128]{1,0:T(1,128)S(1)}, s32[1,128]{1,0:T(1,128)}, u32[]{:S(2)}) copy-start(s32[1,128]{1,0:T(1,128)} %param.21) | copy-start | bytes 1540
  7.2 35.4 %copy-start.8 = (s32[1,128]{1,0:T(1,128)S(1)}, s32[1,128]{1,0:T(1,128)}, u32[]{:S(2)}) copy-start(s32[1,128]{1,0:T(1,128)} %param.22) | copy-start | bytes 1540
  7.2 39.6 %all-gather.3.cloned.1.call-start = ((), (), s32[]{:S(2)}) async-start(), calls=%async_computation.2 | async-start | bytes 1179648 | tf_op jit(solution)/shard_map/all_gather | solution.py:72
  11.4 39.8 %copy-start.4 = (f32[2,1,1,128,128]{4,3,2,1,0:T(8,128)S(1)}, f32[2,1,1,128,128]{4,3,2,1,0:T(8,128)}, u32[]{:S(2)}) copy-start(f32[2,1,1,128,128]{4,3,2,1,0:T(8,128)} %param.23) | copy-start | bytes 393220
  11.4 114.3 %all-to-all-start = ((bf16[1,64,64,2,128]{4,2,3,0,1:T(8,128)(2,1)}), bf16[1,64,64,2,128]{4,2,3,0,1:T(8,128)(2,1)S(1)}, u32[]{:S(2)}, u32[]{:S(2)}) async-start(bf16[1,64,64,2,128]{4,2,3,0,1:T(8,128)(2,1)} %copy.44), calls=%async_computation | async-start | bytes 4194304 | tf_op jit(solution)/shard_map/all_to_all | solution.py:86
  30.7 26.6 %copy-start.6 = (bf16[2,16,128]{2,1,0:T(8,128)(2,1)S(1)}, bf16[2,16,128]{2,1,0:T(8,128)(2,1)}, u32[]{:S(2)}) copy-start(bf16[2,16,128]{2,1,0:T(8,128)(2,1)} %param.18) | copy-start | bytes 24580
  30.7 120.7 %all-gather.5.cloned.1.call-start = ((), (), s32[]{:S(2)}) async-start(), calls=%async_computation.3 | async-start | bytes 2359296 | tf_op jit(solution)/shard_map/all_gather | solution.py:162
  50.6 7.2 %copy-start = (f32[1,512,4,128]{3,1,2,0:T(8,128)}, f32[1,512,4,128]{3,1,2,0:T(8,128)S(1)}, u32[]{:S(2)}) copy-start(f32[1,512,4,128]{3,1,2,0:T(8,128)S(1)} %convolution_bitcast_fusion) | copy-start | bytes 3145732
  57.0 0.7 copy-start.2
  129.9 2.0 %copy-start.1 = (f32[1,512,4,128]{3,1,2,0:T(8,128)S(1)}, f32[1,512,4,128]{3,1,2,0:T(8,128)}, u32[]{:S(2)}) copy-start(f32[1,512,4,128]{3,1,2,0:T(8,128)} %copy-done) | copy-start | bytes 3145732
  129.9 2.5 %copy-start.3 = (f32[512,128]{1,0:T(8,128)S(1)}, f32[512,128]{1,0:T(8,128)}, u32[]{:S(2)}) copy-start(f32[512,128]{1,0:T(8,128)} %copy-done.2) | copy-start | bytes 786436
  135.3 15.9 %all-to-all-start.1 = ((bf16[8,2,4096]{2,1,0:T(2,128)(2,1)}), bf16[8,2,4096]{2,1,0:T(2,128)(2,1)S(1)}, u32[]{:S(2)}, u32[]{:S(2)}) async-start(bf16[8,2,4096]{2,1,0:T(2,128)(2,1)} %reshape.270), calls=%async_computation.1 | async-start | bytes 262144 | tf_op jit(solution)/shard_map/all_to_all | solution.py:160
Sparse Core Ops, SparseCore 0:
  10.2 36.6 all-gather.2
  49.0 32.9 all-gather.4
where the time goes:
time: 162 us; the launch traced here: 161 us
  waiting for transfers between devices  77.3 us (48%)
  starting transfers between devices  29.9 us (18%)
  between operations  22.2 us (14%)
  matrix products  14.8 us (9%)
  local copies, waits for them, and re-layouts  9.12 us (6%)
  other arithmetic  7.67 us (5%)
    all_to_all x1, waiting for transfers between devices, shards(): lax.all_to_all(cache_page_slots, 'req', split_axis=1, concat_axis=0, tile...  67.5 us
    all_to_all x1, starting transfers between devices, shards(): lax.all_to_all(cache_page_slots, 'req', split_axis=1, concat_axis=0, tile...  19.2 us
    all_to_all x1, starting transfers between devices, shards(): lax.all_to_all(mixed_heads, 'head', split_axis=1, concat_axis=2, tiled=True)  10.6 us
    unnamed x26, local copies, waits for them, and re-layouts  6.3 us
    all_to_all x1, waiting for transfers between devices, shards(): lax.all_to_all(mixed_heads, 'head', split_axis=1, concat_axis=2, tiled=True)  4.58 us
    dot_general x16, matrix products, exact_rows(): lax.dot_general(left, right, (((1,), (1,)), ((), ())), precision=lax.Prec...  3.83 us
    all_gather x1, waiting for transfers between devices, shards(): lax.all_gather(tokens, 'head', axis=1, tiled=True).astype(jnp.float32)  3.79 us
  transfers between devices with their start and end apart: 4, of which 3 were waited for; matrix products, arithmetic and copies ran while one was open for 18% of the time, Pallas kernels for 0%

commit v1 on v0

v1 whole, which is shorter than its diff:
```python
import functools
import math

import jax
import jax.numpy as jnp
from jax import lax
from jax.experimental import pallas as pl
from jax.experimental.pallas import tpu as pltpu
from jax.sharding import PartitionSpec as P

HD = 128
BLK = 64
PAGE = 32
NX = 4
CORES = 2
MESH = pl.DeviceIdType.MESH
NEG = -1e30
FLOOR = -5e29
NORM_EPS = 1e-05
UNIT_EPS = 1e-06
HIGHEST = lax.Precision.HIGHEST


def mm(left, right):
    return jnp.dot(left, right, preferred_element_type=jnp.float32)


def exact(left, right):
    return jnp.dot(left, right, precision=HIGHEST, preferred_element_type=jnp.float32)


def soften(scores):
    top = jnp.maximum(jnp.max(scores, axis=0, keepdims=True), FLOOR)
    grown = jnp.exp(scores - top)
    return top, jnp.sum(grown, axis=0, keepdims=True), grown.astype(jnp.bfloat16)


def kernel(
    nz,
    ny,
    tokens_ref,
    gain_ref,
    weight_ref,
    out_weight_ref,
    persist_ref,
    cache_ref,
    length_ref,
    keeper_ref,
    slot_ref,
    state_ref,
    retention_ref,
    momentum_ref,
    stride_ref,
    halving_ref,
    layer_ref,
    new_state_ref,
    tok_buf,
    wout_buf,
    wide,
    w_parts,
    normed,
    kv_buf,
    q_own,
    q_buf,
    fill_own,
    fill_buf,
    keys_own,
    values_t,
    key_unit,
    key_unit_t,
    query_unit_t,
    gate_t,
    read_t,
    mem_m,
    mem_s,
    kv_wide,
    part_acc,
    part_ml,
    send_acc,
    send_ml,
    recv_acc,
    recv_ml,
    home_acc,
    home_ml,
    hout_buf,
    hrecv,
    tok_send,
    tok_recv,
    wo_send,
    wo_recv,
    kv_send,
    kv_recv,
    kv_local,
    q_send,
    q_recv,
    f_send,
    f_recv,
    a_send,
    a_recv,
    m_send,
    m_recv,
    h_send,
    h_recv,
):
    req = lax.axis_index("req")
    head = lax.axis_index("head")
    z, x = req // NX, lax.rem(req, NX)
    y, core = head // CORES, lax.rem(head, CORES)
    heads = ny * CORES
    rows = tokens_ref.shape[0]
    prefill = heads * rows
    half = prefill // 2
    width = tokens_ref.shape[1]
    span = cache_ref.shape[1]
    plane = NX * span // 2
    depth = nz // 2
    scale = 1.0 / math.sqrt(HD)

    partner = y * CORES + (1 - core)
    right_head = lax.rem(y + 1, ny) * CORES + core
    left_head = lax.rem(y + ny - 1, ny) * CORES + core
    anti_head = lax.rem(y + 2, ny) * CORES + core
    z_next = (lax.rem(z + 1, nz) * NX + x, head)
    z_back = (lax.rem(z + nz - 1, nz) * NX + x, head)
    ahead = (z_next, z_back)

    barrier = pltpu.get_barrier_semaphore()
    for peer in ahead:
        pl.semaphore_signal(barrier, inc=1, device_id=peer, device_id_type=MESH)
    for j in range(1, NX):
        peer = (z * NX + lax.rem(x + j, NX), head)
        pl.semaphore_signal(barrier, inc=1, device_id=peer, device_id_type=MESH)
    for j in range(1, heads):
        peer = (req, lax.rem(head + j, heads))
        pl.semaphore_signal(barrier, inc=1, device_id=peer, device_id_type=MESH)
    pl.semaphore_wait(barrier, 2 + NX - 1 + heads - 1)

    def remote(src, dst, send, recv, device):
        return pltpu.make_async_remote_copy(
            src_ref=src,
            dst_ref=dst,
            send_sem=send,
            recv_sem=recv,
            device_id=device,
            device_id_type=MESH,
        )

    def spread(own, buf, send, recv):
        cut = own.shape[0] // 2
        low, high = pl.ds(0, cut), pl.ds(cut, cut)
        to = lambda src, dst, i, k, g: remote(src, dst, send.at[i], recv.at[k], (req, g))
        from_left = buf.at[left_head]
        from_right = buf.at[right_head]
        return (
            to(own, buf.at[head], 0, 0, partner),
            to(own, buf.at[head], 1, 1, right_head),
            to(own, buf.at[head], 2, 2, left_head),
            to(buf.at[left_head, low], buf.at[left_head, low], 3, 3, right_head),
            to(from_left, from_left, 4, 5, partner),
            to(buf.at[right_head, high], buf.at[right_head, high], 5, 4, left_head),
            to(from_right, from_right, 6, 6, partner),
            to(buf.at[anti_head], buf.at[anti_head], 7, 7, partner),
        )

    def spread_mid(c):
        c[1].wait_recv()
        c[3].start()
        c[4].start()
        c[2].wait_recv()
        c[5].start()
        c[6].start()

    def spread_late(c):
        c[3].wait_recv()
        c[5].wait_recv()
        c[7].start()

    tok = spread(tokens_ref, tok_buf, tok_send, tok_recv)
    wout = spread(out_weight_ref, wout_buf, wo_send, wo_recv)
    for c in tok[:3]:
        c.start()

    def kv_copy(rel, j):
        to_x = lax.rem(x + j, NX)
        return remote(
            cache_ref.at[lax.rem(z + rel, nz) * NX + to_x],
            kv_buf.at[rel, x],
            kv_send.at[rel, j - 1],
            kv_recv.at[rel, j - 1],
            (z * NX + to_x, head),
        )

    def kv_stay(rel):
        return pltpu.make_async_copy(
            cache_ref.at[lax.rem(z + rel, nz) * NX + x], kv_buf.at[rel, x], kv_local.at[rel]
        )

    def kv_begin(i, carry):
        sign = 2 * lax.rem(i, 2) - 1
        rel = lax.rem(nz + ((i + 1) // 2) * sign, nz)
        kv_stay(rel).start()
        for j in range(1, NX):
            kv_copy(rel, j).start()
        return carry

    lax.fori_loop(0, nz, kv_begin, 0)

    wide[...] = weight_ref[...].astype(jnp.float32)
    for part in range(4):
        w_parts[part] = wide[pl.ds(part, width, stride=4), :].astype(jnp.bfloat16)

    ids = lax.broadcasted_iota(jnp.int32, (1, 128), 1)
    filled = jnp.clip(length_ref[0] - ids * PAGE, 0, PAGE)
    slot_of = keeper_ref[...] * 2 + slot_ref[...]
    filled_t = jnp.transpose(jnp.broadcast_to(filled.astype(jnp.float32), (128, 128)))
    slot_t = jnp.transpose(jnp.broadcast_to(slot_of.astype(jnp.float32), (128, 128)))
    lanes_f = lax.broadcasted_iota(jnp.int32, (128, 128), 1).astype(jnp.float32)
    slot_fill = jnp.sum(jnp.where(slot_t == lanes_f, filled_t, 0.0), axis=0, keepdims=True)
    fill_own[...] = jnp.broadcast_to(slot_fill, (8, 128))

    def norm_block(block, g):
        x_f = block.astype(jnp.float32)
        mean = jnp.mean(x_f * x_f, axis=-1, keepdims=True)
        scaled = x_f * lax.rsqrt(mean + NORM_EPS) * gain_ref[...].astype(jnp.float32)
        normed[pl.ds(pl.multiple_of(g * rows, rows), rows), :] = scaled.astype(jnp.bfloat16)

    norm_block(tokens_ref[...], head)
    spread_mid(tok)
    tok[0].wait_recv()
    norm_block(tok_buf[partner], partner)
    norm_block(tok_buf[left_head], left_head)
    norm_block(tok_buf[right_head], right_head)
    tok[4].wait_recv()
    flip = lambda g: (g // CORES) * CORES + (1 - core)
    norm_block(tok_buf[flip(left_head)], flip(left_head))
    tok[6].wait_recv()
    norm_block(tok_buf[flip(right_head)], flip(right_head))
    spread_late(tok)
    for c in wout[:3]:
        c.start()
    norm_block(tok_buf[anti_head], anti_head)
    tok[7].wait_recv()
    norm_block(tok_buf[flip(anti_head)], flip(anti_head))

    q_t = jnp.transpose(mm(normed[...], w_parts[0]))
    for h in range(2):
        q_own[h] = q_t[:, h * half : (h + 1) * half].astype(jnp.bfloat16)

    def q_copy(d, h, k):
        src = q_own.at[h] if isinstance(k, int) and k == 0 else q_buf.at[d, k - 1, h]
        return remote(
            src, q_buf.at[d, k, h], q_send.at[d, h, k], q_recv.at[d, h, k], ahead[d]
        )

    def q_done(d, h, k):
        place = q_buf.at[d, k, h]
        return remote(place, place, q_send.at[d, h, k], q_recv.at[d, h, k], ahead[d])

    def f_done(d, k):
        place = fill_buf.at[d, k]
        return remote(place, place, f_send.at[d, k], f_recv.at[d, k], ahead[d])

    def f_copy(d, k):
        src = fill_own if isinstance(k, int) and k == 0 else fill_buf.at[d, k - 1]
        return remote(src, fill_buf.at[d, k], f_send.at[d, k], f_recv.at[d, k], ahead[d])

    for d in range(2):
        f_copy(d, 0).start()
        for h in (d, 1 - d):
            q_copy(d, h, 0).start()

    def unit_columns(v):
        return v * lax.rsqrt(jnp.sum(v * v, axis=0, keepdims=True) + UNIT_EPS)

    for h in range(2):
        query_unit_t[h] = unit_columns(q_own[h].astype(jnp.float32))
    k_bf = mm(normed[...], w_parts[1]).astype(jnp.bfloat16)
    keys_own[...] = k_bf
    k_f = k_bf.astype(jnp.float32)
    k_unit = k_f * lax.rsqrt(jnp.sum(k_f * k_f, axis=-1, keepdims=True) + UNIT_EPS)
    v_bf = mm(normed[...], w_parts[2]).astype(jnp.bfloat16)
    v_t = jnp.transpose(v_bf.astype(jnp.float32))
    k_unit_t = jnp.transpose(k_unit)
    gates = jnp.transpose(mm(normed[...], w_parts[3]))
    values_t[...] = v_t.astype(jnp.bfloat16)
    for b in range(prefill // BLK):
        columns = slice(b * BLK, (b + 1) * BLK)
        key_unit[b] = k_unit[columns, :]
        key_unit_t[b] = jnp.concatenate([k_unit_t[:, columns], v_t[:, columns]], axis=1)
    for h in range(2):
        gate_t[h] = gates[:, h * half : (h + 1) * half]
    mem_m[...] = state_ref[0]
    mem_s[...] = state_ref[1]

    def split_kv(rel):
        kv_stay(rel).wait()
        for j in range(1, NX):
            kv_copy(rel, j).wait_recv()
        for s in range(NX):
            kv_wide[pl.ds(s * span, span), :] = kv_buf[rel, s].astype(jnp.float32)
        keys = kv_wide[pl.ds(0, plane, stride=2), :].astype(jnp.bfloat16)
        vals = jnp.transpose(kv_wide[pl.ds(1, plane, stride=2), :]).astype(jnp.bfloat16)
        return keys, vals

    row_id = lax.broadcasted_iota(jnp.int32, (plane, 128), 0)
    lane_id = lax.broadcasted_iota(jnp.int32, (plane, 128), 1)
    slot_mine = lane_id == z * (NX * 2) + row_id // PAGE
    in_page = lax.rem(row_id[:, 0:1], PAGE).astype(jnp.float32)

    def bias_of(fill_row):
        fills = jnp.sum(jnp.where(slot_mine, fill_row, 0.0), axis=1, keepdims=True)
        return jnp.where(in_page < fills, 0.0, NEG)

    def attend(keys, vals, bias, q):
        top, total, grown = soften(mm(keys, q) * scale + bias)
        return top, total, mm(vals, grown)

    def absorb(d, k, streams, shared=None):
        keys, vals = shared or split_kv(nz - k if d == 0 else k)
        bias = bias_of(fill_buf[d, k - 1][0:1, :])
        for h in streams:
            top, total, acc = attend(keys, vals, bias, q_buf[d, k - 1, h])
            part_acc[d, k - 1, h] = acc
            part_ml[d, k - 1, h, 0:1, :] = top
            part_ml[d, k - 1, h, 1:2, :] = total

    def memory_block(b):
        here = pl.ds(pl.multiple_of(b * BLK, BLK), BLK)
        state = mem_m[...]
        kv = key_unit_t[b]
        errors = exact(state, kv[:, 0:BLK]) - kv[:, BLK:]
        grads = exact(errors, key_unit[b])
        read_t[b] = state
        push = momentum_ref[0, 0] * mem_s[...] - stride_ref[0, 0] * grads
        keep = retention_ref[0, 0] * jnp.where(halving_ref[0, b] == 1, 0.5, 1.0)
        mem_s[...] = push
        mem_m[...] = keep * state + push

    keys0, vals0 = split_kv(0)
    bias0 = bias_of(fill_own[0:1, :])
    for h in range(2):
        count = (h + 1) * half
        q = q_own[h]
        s_c = mm(keys0, q) * scale + bias0
        s_p = mm(persist_ref[0], q) * scale
        s_t = mm(keys_own[0:count, :], q) * scale
        order = lax.broadcasted_iota(jnp.int32, (count, half), 0)
        place = lax.broadcasted_iota(jnp.int32, (count, half), 1) + h * half
        s_t = jnp.where(order <= place, s_t, NEG)
        top_c, total_c, grown_c = soften(s_c)
        top_t, total_t, grown_t = soften(s_t)
        top_p, total_p, grown_p = soften(s_p)
        top = jnp.maximum(jnp.maximum(top_c, top_t), top_p)
        e_c, e_t, e_p = jnp.exp(top_c - top), jnp.exp(top_t - top), jnp.exp(top_p - top)
        persist_t = jnp.transpose(persist_ref[1].astype(jnp.float32)).astype(jnp.bfloat16)
        acc = mm(vals0, grown_c) * e_c + mm(values_t[:, 0:count], grown_t) * e_t
        home_acc[h] = acc + mm(persist_t, grown_p) * e_p
        home_ml[h, 0:1, :] = top
        home_ml[h, 1:2, :] = total_c * e_c + total_t * e_t + total_p * e_p

    def far(d):
        return d

    def gather_step(k, last):
        for d in range(2):
            f_done(d, k - 1).wait_recv()
            f_copy(d, k).start()
            for h in (d, 1 - d):
                q_done(d, h, k - 1).wait_recv()
                if h == far(d) or not last:
                    q_copy(d, h, k).start()

    def gather_loop(k, carry):
        gather_step(k, False)
        memory_block(k - 1)
        for d in range(2):
            absorb(d, k, (0, 1))
        return carry

    lax.fori_loop(1, depth - 1, gather_loop, 0)
    gather_step(depth - 1, True)
    spread_mid(wout)
    for d in range(2):
        absorb(d, depth - 1, (0, 1))

    def ring_copies(d, h, k):
        return (
            remote(
                send_acc.at[d, k, h],
                recv_acc.at[d, k, h],
                a_send.at[d, h, k],
                a_recv.at[d, h, k],
                ahead[1 - d],
            ),
            remote(
                send_ml.at[d, k, h],
                recv_ml.at[d, k, h],
                m_send.at[d, h, k],
                m_recv.at[d, h, k],
                ahead[1 - d],
            ),
        )

    def ring_send(d, h, k, acc, top, total):
        send_acc[d, k, h] = acc.astype(jnp.bfloat16)
        send_ml[d, k, h, 0:1, :] = top
        send_ml[d, k, h, 1:2, :] = total
        for c in ring_copies(d, h, k):
            c.start()

    def join(first, second):
        top = jnp.maximum(first[1], second[1])
        e_a, e_b = jnp.exp(first[1] - top), jnp.exp(second[1] - top)
        return first[0] * e_a + second[0] * e_b, top, first[2] * e_a + second[2] * e_b

    def received(d, h, k):
        for c in ring_copies(d, h, k):
            c.wait_recv()
        return (
            recv_acc[d, k, h].astype(jnp.float32),
            recv_ml[d, k, h, 0:1, :],
            recv_ml[d, k, h, 1:2, :],
        )

    def partial(d, h, k):
        return part_acc[d, k, h], part_ml[d, k, h, 0:1, :], part_ml[d, k, h, 1:2, :]

    def ring_join(d, h, k):
        ring_send(d, h, k, *join(partial(d, h, k), received(d, h, k + 1)))

    last = depth - 1
    opposite = split_kv(depth)
    for d in range(2):
        f_done(d, last).wait_recv()
        q_done(d, far(d), last).wait_recv()
        absorb(d, depth, (far(d),), opposite)
        ring_send(d, far(d), last, *partial(d, far(d), last))
    for d in range(2):
        ring_send(d, 1 - far(d), last - 1, *partial(d, 1 - far(d), last - 1))

    blocks = prefill // BLK

    def memory_rest(b, carry):
        memory_block(b)
        return carry

    lax.fori_loop(depth - 2, blocks, memory_rest, 0)
    new_state_ref[0] = mem_m[...]
    new_state_ref[1] = mem_s[...]
    spread_late(wout)

    def ring_loop(i, carry):
        for d in range(2):
            ring_join(d, far(d), last - i)
        for d in range(2):
            ring_join(d, 1 - far(d), last - 1 - i)
        return carry

    lax.fori_loop(1, last, ring_loop, 0)
    for d in range(2):
        ring_join(d, far(d), 0)

    for b in range(blocks):
        h, place = (b * BLK) // half, (b * BLK) % half
        cols = slice(place, place + BLK)
        gate_t[h, :, cols] = jax.nn.sigmoid(gate_t[h, :, cols]) * exact(
            read_t[b], query_unit_t[h, :, cols]
        )

    def head_copy(j):
        to_head = lax.rem(head + j, heads)
        return remote(
            hout_buf.at[to_head], hrecv.at[j], h_send.at[j], h_recv.at[j], (req, to_head)
        )

    for h in range(2):
        mine = home_acc[h], home_ml[h, 0:1, :], home_ml[h, 1:2, :]
        for d in (1 - h, h):
            mine = join(mine, received(d, h, 0))
        attended = mine[0] / mine[2]
        mean = jnp.mean(attended * attended, axis=0, keepdims=True)
        out = attended * lax.rsqrt(mean + UNIT_EPS) + gate_t[h]
        turned = jnp.transpose(out).astype(jnp.bfloat16)
        per = heads // 2
        for g in range(per):
            hout_buf[h * per + g] = turned[g * rows : (g + 1) * rows, :]

    for j in range(1, heads):
        head_copy(j).start()
    wout[0].wait_recv()
    for i in (4, 6, 7):
        wout[i].wait_recv()
    layer = mm(hout_buf[head], out_weight_ref[...]).astype(jnp.bfloat16).astype(jnp.float32)
    for j in range(1, heads):
        head_copy(j).wait_recv()
        group = lax.rem(head + heads - j, heads)
        layer = layer + mm(hrecv[j], wout_buf[group]).astype(jnp.bfloat16).astype(jnp.float32)
    layer_ref[...] = layer.astype(jnp.bfloat16)

    for c in tok + wout:
        c.wait_send()
    for j in range(1, heads):
        head_copy(j).wait_send()

    def kv_end(rel, carry):
        for j in range(1, NX):
            kv_copy(rel, j).wait_send()
        return carry

    lax.fori_loop(0, nz, kv_end, 0)

    def ring_end(d, h, k):
        q_done(d, h, k).wait_send()
        for c in ring_copies(d, h, k):
            c.wait_send()

    def ends(k, carry):
        for d in range(2):
            f_done(d, k).wait_send()
            for h in range(2):
                ring_end(d, h, k)
        return carry

    lax.fori_loop(0, last, ends, 0)
    for d in range(2):
        f_done(d, last).wait_send()
        ring_end(d, far(d), last)


def shards(
    tokens,
    gain,
    projection_weight,
    output_weight,
    persist,
    cache_page_slots,
    cached_length,
    page_keeper,
    page_slot_index,
    memory_state,
    retention,
    momentum,
    memory_step_scale,
    halving_updates,
    *,
    reqs,
    heads,
):
    nz, ny = reqs // NX, heads // CORES
    depth = nz // 2
    rows, width = tokens.shape[1], tokens.shape[2]
    prefill = rows * heads
    half = prefill // 2
    blocks = prefill // BLK
    span = cache_page_slots.shape[2] * 2
    bf, f32 = jnp.bfloat16, jnp.float32
    vmem = pl.BlockSpec(memory_space=pltpu.VMEM)
    smem = pl.BlockSpec(memory_space=pltpu.SMEM)
    hbm = pl.BlockSpec(memory_space=pl.ANY)
    sems = pltpu.SemaphoreType.DMA
    scratch = [
        pltpu.VMEM((heads, rows, width), bf),
        pltpu.VMEM((heads,) + output_weight.shape, bf),
        pltpu.VMEM((4 * width, HD), f32),
        pltpu.VMEM((4, width, HD), bf),
        pltpu.VMEM((prefill, width), bf),
        pltpu.VMEM((nz, NX, span, HD), bf),
        pltpu.VMEM((2, HD, half), bf),
        pltpu.VMEM((2, depth, 2, HD, half), bf),
        pltpu.VMEM((8, 128), f32),
        pltpu.VMEM((2, depth, 8, 128), f32),
        pltpu.VMEM((prefill, HD), bf),
        pltpu.VMEM((HD, prefill), bf),
        pltpu.VMEM((blocks, BLK, HD), f32),
        pltpu.VMEM((blocks, HD, 2 * BLK), f32),
        pltpu.VMEM((2, HD, half), f32),
        pltpu.VMEM((2, HD, half), f32),
        pltpu.VMEM((blocks, HD, HD), f32),
        pltpu.VMEM((HD, HD), f32),
        pltpu.VMEM((HD, HD), f32),
        pltpu.VMEM((NX * span, HD), f32),
        pltpu.VMEM((2, depth, 2, HD, half), f32),
        pltpu.VMEM((2, depth, 2, 2, half), f32),
        pltpu.VMEM((2, depth, 2, HD, half), bf),
        pltpu.VMEM((2, depth, 2, 2, half), f32),
        pltpu.VMEM((2, depth, 2, HD, half), bf),
        pltpu.VMEM((2, depth, 2, 2, half), f32),
        pltpu.VMEM((2, HD, half), f32),
        pltpu.VMEM((2, 2, half), f32),
        pltpu.VMEM((heads, rows, HD), bf),
        pltpu.VMEM((heads, rows, HD), bf),
        sems((8,)),
        sems((8,)),
        sems((8,)),
        sems((8,)),
        sems((nz, NX)),
        sems((nz, NX)),
        sems((nz,)),
        sems((2, 2, depth)),
        sems((2, 2, depth)),
        sems((2, depth)),
        sems((2, depth)),
        sems((2, 2, depth)),
        sems((2, 2, depth)),
        sems((2, 2, depth)),
        sems((2, 2, depth)),
        sems((heads,)),
        sems((heads,)),
    ]
    layer, state = pl.pallas_call(
        functools.partial(kernel, nz, ny),
        out_shape=(
            jax.ShapeDtypeStruct((rows, width), bf),
            jax.ShapeDtypeStruct((2, HD, HD), f32),
        ),
        in_specs=[vmem, vmem, vmem, vmem, vmem, hbm, smem, vmem, vmem, vmem, smem, smem, smem, smem],
        out_specs=(vmem, vmem),
        scratch_shapes=scratch,
        compiler_params=pltpu.CompilerParams(
            collective_id=0, has_side_effects=True, vmem_limit_bytes=56 * 1024 * 1024
        ),
    )(
        tokens.reshape(rows, width),
        gain.reshape(1, width),
        projection_weight.reshape(4 * width, HD),
        output_weight,
        persist,
        cache_page_slots.reshape(cache_page_slots.shape[1], span, HD),
        cached_length,
        page_keeper,
        page_slot_index,
        memory_state.reshape(2, HD, HD),
        retention,
        momentum,
        memory_step_scale,
        halving_updates,
    )
    return layer.reshape(tokens.shape), state.reshape(memory_state.shape)


def solution(mesh):
    in_specs = (
        P("req", "head", None),
        P(),
        P(None, None, "head"),
        P("head", None),
        P(None, None, "head"),
        P("req", None, None, None, "head"),
        P("req"),
        P("req", None),
        P("req", None),
        P(None, "req", "head", None, None),
        P("req", "head"),
        P("req", "head"),
        P("req", "head"),
        P("req", None),
    )
    out_specs = (P("req", "head", None), P(None, "req", "head", None, None))
    body = functools.partial(shards, reqs=mesh.shape["req"], heads=mesh.shape["head"])
    return jax.shard_map(body, mesh=mesh, in_specs=in_specs, out_specs=out_specs, check_vma=False)
```

time: 162 us -> 108 us (0.67)
  Pallas kernels: 0 us -> 99.8 us
  waiting for transfers between devices: 77.3 us -> 0 us
  starting transfers between devices: 29.9 us -> 0 us
  between operations: 22.2 us -> 3.22 us
  matrix products: 14.8 us -> 0 us
  other arithmetic: 7.67 us -> 0 us
  local copies, waits for them, and re-layouts: 9.12 us -> 4.41 us
    pallas_call x0 -> x1, Pallas kernels: none -> 99.8 us  [shards(): pl.pallas_call(functools.partial(kernel, nz, ny), out_shape=(jax.ShapeDty...]
    all_to_all x2 -> x0, waiting for transfers between devices: 72.1 us -> none  [the longest x1 67.5 us: shards(): lax.all_to_all(cache_page_slots, 'req', split_axis=1, concat_axis=0, tile...]
    all_to_all x2 -> x0, starting transfers between devices: 29.9 us -> none  [the longest x1 19.2 us: shards(): lax.all_to_all(cache_page_slots, 'req', split_axis=1, concat_axis=0, tile...]
    dot_general x32 -> x0, matrix products: 14.8 us -> none  [the longest x16 3.83 us: exact_rows(): lax.dot_general(left, right, (((1,), (1,)), ((), ())), precision=lax.Prec...]
    reduce_sum x8 -> x0, other arithmetic: 5.22 us -> none  [the longest x1 2.15 us: shards(): jnp.sum(exp_c, axis=-1, keepdims=True)]
    all_gather x2 -> x0, waiting for transfers between devices: 3.81 us -> none  [the longest x1 3.79 us: shards(): lax.all_gather(tokens, 'head', axis=1, tiled=True).astype(jnp.float32)]
    unnamed x26 -> x2, local copies, waits for them, and re-layouts: 6.3 us -> 3.14 us
    unnamed x2 -> x0, other arithmetic: 2.07 us -> none
  transfers between devices with their start and end apart: 4 -> 0, of which waited for: 3 -> 0; matrix products, arithmetic and copies ran while one was open for 18% -> 0% of each run, Pallas kernels for 0% -> 0%
where the time goes in v1:
time: 108 us; the launch traced here: 107 us
  Pallas kernels  99.8 us (92%)
  local copies, waits for them, and re-layouts  4.41 us (4%)
  between operations  3.22 us (3%)
    pallas_call x1, Pallas kernels, shards(): pl.pallas_call(functools.partial(kernel, nz, ny), out_shape=(jax.ShapeDty...  99.8 us
    unnamed x2, local copies, waits for them, and re-layouts  3.14 us

profile of v1, /device:TPU:1, one launch (start us, length us, event | category | flops | bytes accessed | tf_op | source)
XLA Modules:
  0.0 107.4 jit_solution(3852995208811004444)
XLA Ops:
  3.2 1.3 %reshape.26.gain_ref = bf16[1,1024]{1,0:T(2,128)(2,1)} reshape(bf16[1024]{0:T(1024)(128)(2,1)} %param.15) | data formatting | bytes 4096 | tf_op jit(solution)/shard_map/reshape | solution.py:624
  4.5 99.8 %shard_map.149 = (bf16[64,1024]{1,0:T(8,128)(2,1)}, f32[2,128,128]{2,1,0:T(8,128)}) custom-call(bf16[64,1024]{1,0:T(8,128)(2,1)} %bitcast.10, bf16[1,1024]{1,0:T(2,128)(2,1)} %reshape.26.gain_ref, bf16[4096,128]{1,0:T(8,128)(2,1)} %bitcast.9, bf16[128,1024]{1,0:T(8,128)(2,1)} %out_weight_ref.1, bf16[2,16,128]{2,1,0:T(8,128)(2,1)} %persist_ref.1, ...), custom_call_target="tpu_custom_call" | custom-call | tf_op jit(solution)/shard_map/pallas_call | solution.py:610
  104.3 1.6 %copy.23 = bf16[1,64,1024]{2,1,0:T(8,128)(2,1)} copy(bf16[1,64,1024]{2,1,0:T(8,128)(2,1)} %bitcast.13) | data formatting | bytes 262144
  105.8 1.6 %copy.24 = f32[2,1,1,128,128]{4,3,2,1,0:T(8,128)} copy(f32[2,1,1,128,128]{4,3,2,1,0:T(8,128)} %bitcast.12) | data formatting | bytes 262144

commit v2 on v1

v2 whole, which is shorter than its diff:
```python
import functools
import math

import jax
import jax.numpy as jnp
from jax import lax
from jax.experimental import pallas as pl
from jax.experimental.pallas import tpu as pltpu
from jax.sharding import PartitionSpec as P

HD = 128
BLK = 64
PAGE = 32
NX = 4
CORES = 2
REACH = 5
MESH = pl.DeviceIdType.MESH
NEG = -1e30
FLOOR = -5e29
NORM_EPS = 1e-05
UNIT_EPS = 1e-06
HIGHEST = lax.Precision.HIGHEST


def mm(left, right):
    return jnp.dot(left, right, preferred_element_type=jnp.float32)


def exact(left, right):
    return jnp.dot(left, right, precision=HIGHEST, preferred_element_type=jnp.float32)


def soften(scores):
    top = jnp.maximum(jnp.max(scores, axis=0, keepdims=True), FLOOR)
    grown = jnp.exp(scores - top)
    return top, jnp.sum(grown, axis=0, keepdims=True), grown.astype(jnp.bfloat16)


def kernel(
    nz,
    ny,
    tokens_ref,
    gain_ref,
    weight_ref,
    out_weight_ref,
    persist_ref,
    cache_ref,
    length_ref,
    keeper_ref,
    slot_ref,
    state_ref,
    retention_ref,
    momentum_ref,
    stride_ref,
    halving_ref,
    layer_ref,
    new_state_ref,
    tok_buf,
    wout_buf,
    wide,
    w_parts,
    normed,
    kv_home,
    kv_buf,
    q_own,
    q_buf,
    fill_own,
    fill_buf,
    keys_own,
    values_t,
    key_unit,
    key_unit_t,
    value_f,
    query_unit_t,
    gate_t,
    extra_t,
    mem_m,
    mem_s,
    kv_wide,
    keys_far,
    values_far,
    part_acc,
    part_ml,
    send_acc,
    send_ml,
    recv_acc,
    recv_ml,
    home_acc,
    home_ml,
    hout_buf,
    hrecv,
    tok_send,
    tok_recv,
    wo_send,
    wo_recv,
    h0_send,
    h0_recv,
    h0_local,
    kv_send,
    kv_recv,
    kv_local,
    q_send,
    q_recv,
    f_send,
    f_recv,
    a_send,
    a_recv,
    m_send,
    m_recv,
    h_send,
    h_recv,
):
    req = lax.axis_index("req")
    head = lax.axis_index("head")
    z, x = req // NX, lax.rem(req, NX)
    y, core = head // CORES, lax.rem(head, CORES)
    heads = ny * CORES
    rows = tokens_ref.shape[0]
    prefill = heads * rows
    half = prefill // 2
    width = tokens_ref.shape[1]
    span = cache_ref.shape[1]
    plane = NX * span // 2
    depth = nz // 2
    reach = min(REACH, depth - 1)
    beyond = depth - reach
    scale = 1.0 / math.sqrt(HD)

    partner = y * CORES + (1 - core)
    right_head = lax.rem(y + 1, ny) * CORES + core
    left_head = lax.rem(y + ny - 1, ny) * CORES + core
    anti_head = lax.rem(y + 2, ny) * CORES + core
    z_next = (lax.rem(z + 1, nz) * NX + x, head)
    z_back = (lax.rem(z + nz - 1, nz) * NX + x, head)
    ahead = (z_next, z_back)

    barrier = pltpu.get_barrier_semaphore()
    for hop in range(-beyond, beyond + 1):
        for j in range(NX):
            if hop or j:
                peer = (lax.rem(z + nz + hop, nz) * NX + lax.rem(x + j, NX), head)
                pl.semaphore_signal(barrier, inc=1, device_id=peer, device_id_type=MESH)
    for j in range(1, heads):
        peer = (req, lax.rem(head + j, heads))
        pl.semaphore_signal(barrier, inc=1, device_id=peer, device_id_type=MESH)
    pl.semaphore_wait(barrier, (2 * beyond + 1) * NX - 1 + heads - 1)

    def remote(src, dst, send, recv, device):
        return pltpu.make_async_remote_copy(
            src_ref=src,
            dst_ref=dst,
            send_sem=send,
            recv_sem=recv,
            device_id=device,
            device_id_type=MESH,
        )

    def spread(own, buf, send, recv):
        cut = own.shape[0] // 2
        low, high = pl.ds(0, cut), pl.ds(cut, cut)
        to = lambda src, dst, i, g: remote(src, dst, send.at[i], recv.at[i], (req, g))
        from_left = buf.at[left_head]
        from_right = buf.at[right_head]
        mine = buf.at[head]
        return (
            to(own, mine, 0, partner),
            to(own.at[low], buf.at[head, low], 1, right_head),
            to(own.at[high], buf.at[head, high], 2, right_head),
            to(own.at[low], buf.at[head, low], 3, left_head),
            to(own.at[high], buf.at[head, high], 4, left_head),
            to(buf.at[left_head, low], buf.at[left_head, low], 5, right_head),
            to(buf.at[right_head, high], buf.at[right_head, high], 6, left_head),
            to(from_left, from_left, 7, partner),
            to(from_right, from_right, 8, partner),
            to(buf.at[anti_head, low], buf.at[anti_head, low], 9, partner),
            to(buf.at[anti_head, high], buf.at[anti_head, high], 10, partner),
        )

    def spread_begin(c):
        for i in (1, 4, 0, 2, 3):
            c[i].start()

    def spread_mid(c):
        for first, then in ((1, 5), (4, 6), (2, 7), (3, 8)):
            c[first].wait_recv()
            c[then].start()

    def spread_late(c):
        for first, then in ((5, 9), (6, 10)):
            c[first].wait_recv()
            c[then].start()

    tok = spread(tokens_ref, tok_buf, tok_send, tok_recv)
    wout = spread(out_weight_ref, wout_buf, wo_send, wo_recv)
    spread_begin(tok)

    def home_copy(j):
        to_x = lax.rem(x + j, NX)
        return remote(
            cache_ref.at[z * NX + to_x],
            kv_home.at[x],
            h0_send.at[j],
            h0_recv.at[j],
            (z * NX + to_x, head),
        )

    def home_stay():
        return pltpu.make_async_copy(cache_ref.at[req], kv_home.at[x], h0_local)

    def kv_copy(d, k, j):
        sign = 1 - 2 * d
        to_x = lax.rem(x + j, NX)
        asker = lax.rem(z + nz - sign * k, nz)
        over = max(k - reach, 0) if isinstance(k, int) else 0
        server = lax.rem(z + nz - sign * over, nz)
        return remote(
            cache_ref.at[asker * NX + to_x],
            kv_buf.at[d, k - 1, x],
            kv_send.at[d, k - 1, j],
            kv_recv.at[d, k - 1, j],
            (server * NX + to_x, head),
        )

    def kv_stay(d, k):
        asker = lax.rem(z + nz - (1 - 2 * d) * k, nz)
        return pltpu.make_async_copy(
            cache_ref.at[asker * NX + x], kv_buf.at[d, k - 1, x], kv_local.at[d, k - 1]
        )

    side = x // (NX // 2)
    for j in range(NX):
        kv_copy(side, depth, j).start()
    for k in range(depth - 1, reach, -1):
        for d in range(2):
            for j in range(NX):
                kv_copy(d, k, j).start()

    wide[...] = weight_ref[...].astype(jnp.float32)
    for part in range(4):
        w_parts[part] = wide[pl.ds(part, width, stride=4), :].astype(jnp.bfloat16)

    spread_mid(tok)
    for k in range(1, reach + 1):
        for d in range(2):
            kv_stay(d, k).start()
            for j in range(1, NX):
                kv_copy(d, k, j).start()
    home_stay().start()
    for j in range(1, NX):
        home_copy(j).start()

    ids = lax.broadcasted_iota(jnp.int32, (1, 128), 1)
    filled = jnp.clip(length_ref[0] - ids * PAGE, 0, PAGE).astype(jnp.float32)
    slot_of = keeper_ref[...] * 2 + slot_ref[...]
    filled_t = jnp.transpose(jnp.broadcast_to(filled, (128, 128)))
    slot_t = jnp.transpose(jnp.broadcast_to(slot_of.astype(jnp.float32), (128, 128)))
    lanes_f = lax.broadcasted_iota(jnp.int32, (128, 128), 1).astype(jnp.float32)
    slot_fill = jnp.sum(jnp.where(slot_t == lanes_f, filled_t, 0.0), axis=0, keepdims=True)
    fill_own[...] = jnp.broadcast_to(slot_fill, (8, 128))

    gain_f = gain_ref[...].astype(jnp.float32)
    gain_row = jnp.concatenate([gain_f[i : i + 1, :] for i in range(width // 128)], axis=1)

    def norm_block(block, g):
        x_f = block.astype(jnp.float32)
        mean = jnp.mean(x_f * x_f, axis=-1, keepdims=True)
        scaled = x_f * lax.rsqrt(mean + NORM_EPS) * gain_row
        normed[pl.ds(pl.multiple_of(g * rows, rows), rows), :] = scaled.astype(jnp.bfloat16)

    norm_block(tokens_ref[...], head)
    norm_block(tok_buf[left_head], left_head)
    norm_block(tok_buf[right_head], right_head)
    spread_late(tok)
    spread_begin(wout)
    norm_block(tok_buf[anti_head], anti_head)
    tok[0].wait_recv()
    norm_block(tok_buf[partner], partner)
    flip = lambda g: (g // CORES) * CORES + (1 - core)
    for i, g in ((7, left_head), (8, right_head)):
        tok[i].wait_recv()
        norm_block(tok_buf[flip(g)], flip(g))
    tok[9].wait_recv()
    tok[10].wait_recv()
    norm_block(tok_buf[flip(anti_head)], flip(anti_head))

    q_t = jnp.transpose(mm(normed[...], w_parts[0]))
    for h in range(2):
        q_own[h] = q_t[:, h * half : (h + 1) * half].astype(jnp.bfloat16)

    def q_copy(d, h, k):
        src = q_own.at[h] if isinstance(k, int) and k == 0 else q_buf.at[d, k - 1, h]
        return remote(
            src, q_buf.at[d, k, h], q_send.at[d, h, k], q_recv.at[d, h, k], ahead[d]
        )

    def q_done(d, h, k):
        place = q_buf.at[d, k, h]
        return remote(place, place, q_send.at[d, h, k], q_recv.at[d, h, k], ahead[d])

    def f_done(d, k):
        place = fill_buf.at[d, k]
        return remote(place, place, f_send.at[d, k], f_recv.at[d, k], ahead[d])

    def f_copy(d, k):
        src = fill_own if isinstance(k, int) and k == 0 else fill_buf.at[d, k - 1]
        return remote(src, fill_buf.at[d, k], f_send.at[d, k], f_recv.at[d, k], ahead[d])

    for d in range(2):
        f_copy(d, 0).start()
        for h in (d, 1 - d):
            q_copy(d, h, 0).start()

    def unit_columns(v):
        return v * lax.rsqrt(jnp.sum(v * v, axis=0, keepdims=True) + UNIT_EPS)

    k_bf = mm(normed[...], w_parts[1]).astype(jnp.bfloat16)
    keys_own[...] = k_bf
    k_f = k_bf.astype(jnp.float32)
    k_unit = k_f * lax.rsqrt(jnp.sum(k_f * k_f, axis=-1, keepdims=True) + UNIT_EPS)
    v_bf = mm(normed[...], w_parts[2]).astype(jnp.bfloat16)
    v_t = jnp.transpose(v_bf.astype(jnp.float32))
    k_unit_t = jnp.transpose(k_unit)
    gates = jnp.transpose(mm(normed[...], w_parts[3]))
    values_t[...] = v_t.astype(jnp.bfloat16)
    units = unit_columns(jnp.concatenate([q_own[0], q_own[1]], axis=1).astype(jnp.float32))
    for b in range(prefill // BLK):
        key_unit[b] = k_unit[b * BLK : (b + 1) * BLK, :]
    for p in range(prefill // (2 * BLK)):
        columns = slice(p * 2 * BLK, (p + 1) * 2 * BLK)
        key_unit_t[p] = k_unit_t[:, columns]
        value_f[p] = v_t[:, columns]
        query_unit_t[p] = units[:, columns]
        gate_t[p] = gates[:, columns]
    mem_m[...] = state_ref[0]
    mem_s[...] = state_ref[1]

    def pick(blocks):
        count = len(blocks) * span
        for s, block in enumerate(blocks):
            kv_wide[s * span : (s + 1) * span, :] = block.astype(jnp.float32)
        keys = kv_wide[pl.ds(0, count // 2, stride=2), :].astype(jnp.bfloat16)
        vals = jnp.transpose(kv_wide[pl.ds(1, count // 2, stride=2), :]).astype(jnp.bfloat16)
        return keys, vals

    def split_near(d, k):
        kv_stay(d, k).wait()
        for j in range(1, NX):
            kv_copy(d, k, j).wait_recv()
        return pick([kv_buf[d, k - 1, s] for s in range(NX)])

    far_sides = tuple(tuple(range(d * NX // 2, (d + 1) * NX // 2)) for d in range(2))
    far_rows = (beyond + 1) * plane - plane // 2

    def split_far(d):
        for k in range(reach, depth + 1):
            if k == reach:
                keys, vals = split_near(d, k)
            elif k < depth:
                for j in range(NX):
                    kv_copy(d, k, j).wait_recv()
                keys, vals = pick([kv_buf[d, k - 1, s] for s in range(NX)])
            else:
                for s in far_sides[d]:
                    kv_copy(d, k, lax.rem(x + NX - s, NX)).wait_recv()
                keys, vals = pick([kv_buf[d, k - 1, s] for s in far_sides[d]])
            at = (k - reach) * plane
            keys_far[d, at : at + keys.shape[0], :] = keys
            values_far[d, :, at : at + keys.shape[0]] = vals

    def bias_of(fill_row, server, first, count):
        row_id = lax.broadcasted_iota(jnp.int32, (count, 128), 0)
        lane_id = lax.broadcasted_iota(jnp.int32, (count, 128), 1)
        slot_mine = lane_id == server * (NX * 2) + first + row_id // PAGE
        fills = jnp.sum(jnp.where(slot_mine, fill_row, 0.0), axis=1, keepdims=True)
        in_page = lax.rem(row_id[:, 0:1], PAGE).astype(jnp.float32)
        return jnp.where(in_page < fills, 0.0, NEG)

    def attend(keys, vals, bias, q):
        top, total, grown = soften(mm(keys, q) * scale + bias)
        return top, total, mm(vals, grown)

    def keep_part(d, k, h, result):
        top, total, acc = result
        part_acc[d, k - 1, h] = acc
        part_ml[d, k - 1, h, 0:1, :] = top
        part_ml[d, k - 1, h, 1:2, :] = total

    def absorb(d, k):
        keys, vals = split_near(d, k)
        bias = bias_of(fill_buf[d, k - 1][0:1, :], z, 0, plane)
        for h in range(2):
            keep_part(d, k, h, attend(keys, vals, bias, q_buf[d, k - 1, h]))

    def memory_pair(p):
        reads = []
        for u in range(2):
            columns = slice(u * BLK, (u + 1) * BLK)
            b = 2 * p + u
            state = mem_m[...]
            reads.append(exact(state, query_unit_t[p][:, columns]))
            errors = exact(state, key_unit_t[p][:, columns]) - value_f[p][:, columns]
            grads = exact(errors, key_unit[b])
            push = momentum_ref[0, 0] * mem_s[...] - stride_ref[0, 0] * grads
            keep = retention_ref[0, 0] * jnp.where(halving_ref[0, b] == 1, 0.5, 1.0)
            mem_s[...] = push
            mem_m[...] = keep * state + push
        extra_t[p] = jax.nn.sigmoid(gate_t[p]) * jnp.concatenate(reads, axis=1)

    def own_attention():
        home_stay().wait()
        for j in range(1, NX):
            home_copy(j).wait_recv()
        keys0, vals0 = pick([kv_home[s] for s in range(NX)])
        bias0 = bias_of(fill_own[0:1, :], z, 0, plane)
        persist_t = jnp.transpose(persist_ref[1].astype(jnp.float32)).astype(jnp.bfloat16)
        for h in range(2):
            count = (h + 1) * half
            q = q_own[h]
            s_c = mm(keys0, q) * scale + bias0
            s_p = mm(persist_ref[0], q) * scale
            s_t = mm(keys_own[0:count, :], q) * scale
            order = lax.broadcasted_iota(jnp.int32, (count, half), 0)
            place = lax.broadcasted_iota(jnp.int32, (count, half), 1) + h * half
            s_t = jnp.where(order <= place, s_t, NEG)
            top_c, total_c, grown_c = soften(s_c)
            top_t, total_t, grown_t = soften(s_t)
            top_p, total_p, grown_p = soften(s_p)
            top = jnp.maximum(jnp.maximum(top_c, top_t), top_p)
            e_c, e_t, e_p = jnp.exp(top_c - top), jnp.exp(top_t - top), jnp.exp(top_p - top)
            acc = mm(vals0, grown_c) * e_c + mm(values_t[:, 0:count], grown_t) * e_t
            home_acc[h] = acc + mm(persist_t, grown_p) * e_p
            home_ml[h, 0:1, :] = top
            home_ml[h, 1:2, :] = total_c * e_c + total_t * e_t + total_p * e_p

    order_of = lambda d: (d, 1 - d)

    def gather_step(k):
        for d in range(2):
            f_done(d, k - 1).wait_recv()
            f_copy(d, k).start()
            for h in order_of(d):
                q_done(d, h, k - 1).wait_recv()
                q_copy(d, h, k).start()

    for d in range(2):
        split_far(d)

    def gather_loop(k, carry):
        gather_step(k)
        for d in range(2):
            absorb(d, k)
        return carry

    lax.fori_loop(1, reach, gather_loop, 0)
    spread_mid(wout)

    def ring_copies(d, h, k):
        return (
            remote(
                send_acc.at[d, k, h],
                recv_acc.at[d, k, h],
                a_send.at[d, h, k],
                a_recv.at[d, h, k],
                ahead[1 - d],
            ),
            remote(
                send_ml.at[d, k, h],
                recv_ml.at[d, k, h],
                m_send.at[d, h, k],
                m_recv.at[d, h, k],
                ahead[1 - d],
            ),
        )

    def ring_send(d, h, k, acc, top, total):
        send_acc[d, k, h] = acc.astype(jnp.bfloat16)
        send_ml[d, k, h, 0:1, :] = top
        send_ml[d, k, h, 1:2, :] = total
        for c in ring_copies(d, h, k):
            c.start()

    def join(first, second):
        top = jnp.maximum(first[1], second[1])
        e_a, e_b = jnp.exp(first[1] - top), jnp.exp(second[1] - top)
        return first[0] * e_a + second[0] * e_b, top, first[2] * e_a + second[2] * e_b

    def received(d, h, k):
        for c in ring_copies(d, h, k):
            c.wait_recv()
        return (
            recv_acc[d, k, h].astype(jnp.float32),
            recv_ml[d, k, h, 0:1, :],
            recv_ml[d, k, h, 1:2, :],
        )

    def partial(d, h, k):
        return part_acc[d, k, h], part_ml[d, k, h, 0:1, :], part_ml[d, k, h, 1:2, :]

    def ring_join(d, h, k):
        ring_send(d, h, k, *join(partial(d, h, k), received(d, h, k + 1)))

    last = reach - 1
    biases = []
    for d in range(2):
        f_done(d, last).wait_recv()
        fill_row = fill_buf[d, last][0:1, :]
        pieces = []
        for hop in range(beyond + 1):
            server = lax.rem(z + nz + (1 - 2 * d) * hop, nz)
            first, count = (d * NX, plane // 2) if hop == beyond else (0, plane)
            pieces.append(bias_of(fill_row, server, first, count))
        biases.append(jnp.concatenate(pieces, axis=0))
    for i in range(2):
        for d in range(2):
            h = order_of(d)[i]
            q_done(d, h, last).wait_recv()
            top, total, acc = attend(
                keys_far[d], values_far[d], biases[d], q_buf[d, last, h]
            )
            ring_send(d, h, last, acc, top, total)

    own_attention()
    spread_late(wout)
    pairs = prefill // (2 * BLK)

    def ring_loop(i, carry):
        for n in range(2):
            for d in range(2):
                ring_join(d, order_of(d)[n], last - i)
        pl.when(i <= pairs)(lambda: memory_pair(i - 1))
        return carry

    lax.fori_loop(1, reach, ring_loop, 0)
    for p in range(reach - 1, pairs):
        memory_pair(p)
    new_state_ref[0] = mem_m[...]
    new_state_ref[1] = mem_s[...]

    def head_copy(g):
        return remote(hout_buf.at[g], hrecv.at[head], h_send.at[g], h_recv.at[head], (req, g))

    def head_arrival(g):
        return remote(hout_buf.at[g], hrecv.at[g], h_send.at[g], h_recv.at[g], (req, g))

    per = heads // 2
    for h in range(2):
        mine = home_acc[h], home_ml[h, 0:1, :], home_ml[h, 1:2, :]
        for d in (h, 1 - h):
            mine = join(mine, received(d, h, 0))
        attended = mine[0] / mine[2]
        mean = jnp.mean(attended * attended, axis=0, keepdims=True)
        some = pairs // 2
        extra = jnp.concatenate([extra_t[h * some + p] for p in range(some)], axis=1)
        out = attended * lax.rsqrt(mean + UNIT_EPS) + extra
        turned = jnp.transpose(out).astype(jnp.bfloat16)
        for g in range(h * per, (h + 1) * per):
            hout_buf[g] = turned[(g - h * per) * rows : (g - h * per + 1) * rows, :]
        for g in range(h * per, (h + 1) * per):
            pl.when(g != head)(lambda g=g: head_copy(g).start())

    for i in (0, 7, 8, 9, 10):
        wout[i].wait_recv()
    layer = mm(hout_buf[head], out_weight_ref[...]).astype(jnp.bfloat16).astype(jnp.float32)
    for j in range(1, heads):
        group = lax.rem(head + j, heads)
        head_arrival(group).wait_recv()
        layer = layer + mm(hrecv[group], wout_buf[group]).astype(jnp.bfloat16).astype(jnp.float32)
    layer_ref[...] = layer.astype(jnp.bfloat16)

    for c in tok + wout:
        c.wait_send()
    for j in range(1, heads):
        head_copy(lax.rem(head + j, heads)).wait_send()
    for j in range(1, NX):
        home_copy(j).wait_send()
        for k in range(1, reach + 1):
            for d in range(2):
                kv_copy(d, k, j).wait_send()
    for j in range(NX):
        for k in range(reach + 1, depth):
            for d in range(2):
                kv_copy(d, k, j).wait_send()
        kv_copy(side, depth, j).wait_send()

    def ends(k, carry):
        for d in range(2):
            f_done(d, k).wait_send()
            for h in range(2):
                q_done(d, h, k).wait_send()
                for c in ring_copies(d, h, k):
                    c.wait_send()
        return carry

    lax.fori_loop(0, reach, ends, 0)


def settle(layer_ref, state_ref, layer_out, state_out):
    layer_out[...] = layer_ref[...]
    state_out[...] = state_ref[...]


def shards(
    tokens,
    gain,
    projection_weight,
    output_weight,
    persist,
    cache_page_slots,
    cached_length,
    page_keeper,
    page_slot_index,
    memory_state,
    retention,
    momentum,
    memory_step_scale,
    halving_updates,
    *,
    reqs,
    heads,
):
    nz, ny = reqs // NX, heads // CORES
    depth = nz // 2
    rows, width = tokens.shape[1], tokens.shape[2]
    prefill = rows * heads
    half = prefill // 2
    blocks = prefill // BLK
    span = cache_page_slots.shape[2] * 2
    bf, f32 = jnp.bfloat16, jnp.float32
    vmem = pl.BlockSpec(memory_space=pltpu.VMEM)
    smem = pl.BlockSpec(memory_space=pltpu.SMEM)
    hbm = pl.BlockSpec(memory_space=pl.ANY)
    sems = pltpu.SemaphoreType.DMA
    reach = min(REACH, depth - 1)
    pairs = blocks // 2
    rings = (2, reach, 2)
    far_rows = (depth - reach + 1) * NX * span // 2 - NX * span // 4
    scratch = [
        pltpu.VMEM((heads, rows, width), bf),
        pltpu.VMEM((heads,) + output_weight.shape, bf),
        pltpu.VMEM((4 * width, HD), f32),
        pltpu.VMEM((4, width, HD), bf),
        pltpu.VMEM((prefill, width), bf),
        pltpu.VMEM((NX, span, HD), bf),
        pltpu.VMEM((2, depth, NX, span, HD), bf),
        pltpu.VMEM((2, HD, half), bf),
        pltpu.VMEM(rings + (HD, half), bf),
        pltpu.VMEM((8, 128), f32),
        pltpu.VMEM((2, reach, 8, 128), f32),
        pltpu.VMEM((prefill, HD), bf),
        pltpu.VMEM((HD, prefill), bf),
        pltpu.VMEM((blocks, BLK, HD), f32),
        pltpu.VMEM((pairs, HD, 2 * BLK), f32),
        pltpu.VMEM((pairs, HD, 2 * BLK), f32),
        pltpu.VMEM((pairs, HD, 2 * BLK), f32),
        pltpu.VMEM((pairs, HD, 2 * BLK), f32),
        pltpu.VMEM((pairs, HD, 2 * BLK), f32),
        pltpu.VMEM((HD, HD), f32),
        pltpu.VMEM((HD, HD), f32),
        pltpu.VMEM((NX * span, HD), f32),
        pltpu.VMEM((2, far_rows, HD), bf),
        pltpu.VMEM((2, HD, far_rows), bf),
        pltpu.VMEM(rings + (HD, half), f32),
        pltpu.VMEM(rings + (2, half), f32),
        pltpu.VMEM(rings + (HD, half), bf),
        pltpu.VMEM(rings + (2, half), f32),
        pltpu.VMEM(rings + (HD, half), bf),
        pltpu.VMEM(rings + (2, half), f32),
        pltpu.VMEM((2, HD, half), f32),
        pltpu.VMEM((2, 2, half), f32),
        pltpu.VMEM((heads, rows, HD), bf),
        pltpu.VMEM((heads, rows, HD), bf),
        sems((11,)),
        sems((11,)),
        sems((11,)),
        sems((11,)),
        sems((NX,)),
        sems((NX,)),
        sems,
        sems((2, depth, NX)),
        sems((2, depth, NX)),
        sems((2, depth)),
        sems((2, 2, reach)),
        sems((2, 2, reach)),
        sems((2, reach)),
        sems((2, reach)),
        sems((2, 2, reach)),
        sems((2, 2, reach)),
        sems((2, 2, reach)),
        sems((2, 2, reach)),
        sems((heads,)),
        sems((heads,)),
    ]
    layer, state = pl.pallas_call(
        functools.partial(kernel, nz, ny),
        out_shape=(
            jax.ShapeDtypeStruct((rows, width), bf),
            jax.ShapeDtypeStruct((2, HD, HD), f32),
        ),
        in_specs=[vmem] * 5 + [hbm, smem, vmem, vmem, vmem] + [smem] * 4,
        out_specs=(vmem, vmem),
        scratch_shapes=scratch,
        compiler_params=pltpu.CompilerParams(
            collective_id=0, has_side_effects=True, vmem_limit_bytes=56 * 1024 * 1024
        ),
    )(
        tokens.reshape(rows, width),
        gain.reshape(width // 128, 128),
        projection_weight.reshape(4 * width, HD),
        output_weight,
        persist,
        cache_page_slots.reshape(cache_page_slots.shape[1], span, HD),
        cached_length,
        page_keeper,
        page_slot_index,
        memory_state.reshape(2, HD, HD),
        retention,
        momentum,
        memory_step_scale,
        halving_updates,
    )
    layer, state = pl.pallas_call(
        settle,
        out_shape=(
            jax.ShapeDtypeStruct((rows, width), bf),
            jax.ShapeDtypeStruct((2, HD, HD), f32),
        ),
        in_specs=[vmem, vmem],
        out_specs=(vmem, vmem),
    )(layer, state)
    return layer.reshape(tokens.shape), state.reshape(memory_state.shape)


def solution(mesh):
    in_specs = (
        P("req", "head", None),
        P(),
        P(None, None, "head"),
        P("head", None),
        P(None, None, "head"),
        P("req", None, None, None, "head"),
        P("req"),
        P("req", None),
        P("req", None),
        P(None, "req", "head", None, None),
        P("req", "head"),
        P("req", "head"),
        P("req", "head"),
        P("req", None),
    )
    out_specs = (P("req", "head", None), P(None, "req", "head", None, None))
    body = functools.partial(shards, reqs=mesh.shape["req"], heads=mesh.shape["head"])
    return jax.shard_map(body, mesh=mesh, in_specs=in_specs, out_specs=out_specs, check_vma=False)
```

time: 108 us -> 97.3 us (0.901)
  Pallas kernels: 99.8 us -> 93.9 us
  local copies, waits for them, and re-layouts: 4.41 us -> 0 us
    pallas_call x1, Pallas kernels: 99.8 us -> 92.2 us  [shards(): pl.pallas_call(functools.partial(kernel, nz, ny), out_shape=(jax.ShapeDty...]
    unnamed x2 -> x0, local copies, waits for them, and re-layouts: 3.14 us -> none
    pallas_call x0 -> x1, Pallas kernels: none -> 1.68 us  [shards(): pl.pallas_call(settle, out_shape=(jax.ShapeDtypeStruct((rows, width), bf)...]
    reshape x1 -> x0, local copies, waits for them, and re-layouts: 1.28 us -> none  [shards(): gain.reshape(1, width)]
where the time goes in v2:
time: 97.3 us; the launch traced here: 97.1 us
  Pallas kernels  93.9 us (97%)
  between operations  3.22 us (3%)
    pallas_call x1, Pallas kernels, shards(): pl.pallas_call(functools.partial(kernel, nz, ny), out_shape=(jax.ShapeDty...  92.2 us

profile of v2, /device:TPU:1, one launch (start us, length us, event | category | flops | bytes accessed | tf_op | source)
XLA Modules:
  0.0 97.1 jit_solution(4594699926765647866)
XLA Ops:
  3.2 92.2 %shard_map.149 = (bf16[64,1024]{1,0:T(8,128)(2,1)}, f32[2,128,128]{2,1,0:T(8,128)}) custom-call(bf16[64,1024]{1,0:T(8,128)(2,1)} %bitcast.11, bf16[8,128]{1,0:T(8,128)(2,1)} %bitcast.13, bf16[4096,128]{1,0:T(8,128)(2,1)} %bitcast.10, bf16[128,1024]{1,0:T(8,128)(2,1)} %out_weight_ref.1, bf16[2,16,128]{2,1,0:T(8,128)(2,1)} %persist_ref.1, ...), custom_call_target="tpu_custom_call" | custom-call | tf_op jit(solution)/shard_map/pallas_call | solution.py:693
  95.4 1.7 %shard_map.150 = (bf16[64,1024]{1,0:T(8,128)(2,1)}, f32[2,128,128]{2,1,0:T(8,128)}) custom-call(bf16[64,1024]{1,0:T(8,128)(2,1)} %get-tuple-element.6.layer_ref, f32[2,128,128]{2,1,0:T(8,128)} %get-tuple-element.7.state_ref), custom_call_target="tpu_custom_call" | custom-call | tf_op jit(solution)/shard_map/pallas_call | solution.py:721

commit v3 on v2

--- a/solution.py
+++ b/solution.py
@@ -14,6 +14,7 @@
 NX = 4
 CORES = 2
 REACH = 5
+CHUNK = 128
 MESH = pl.DeviceIdType.MESH
 NEG = -1e30
 FLOOR = -5e29
@@ -117,7 +118,7 @@
     heads = ny * CORES
     rows = tokens_ref.shape[0]
     prefill = heads * rows
-    half = prefill // 2
+    chunks = prefill // CHUNK
     width = tokens_ref.shape[1]
     span = cache_ref.shape[1]
     plane = NX * span // 2
@@ -227,9 +228,8 @@
             cache_ref.at[asker * NX + x], kv_buf.at[d, k - 1, x], kv_local.at[d, k - 1]
         )
 
-    side = x // (NX // 2)
     for j in range(NX):
-        kv_copy(side, depth, j).start()
+        kv_copy(j % 2, depth, j).start()
     for k in range(depth - 1, reach, -1):
         for d in range(2):
             for j in range(NX):
@@ -284,8 +284,8 @@
     norm_block(tok_buf[flip(anti_head)], flip(anti_head))
 
     q_t = jnp.transpose(mm(normed[...], w_parts[0]))
-    for h in range(2):
-        q_own[h] = q_t[:, h * half : (h + 1) * half].astype(jnp.bfloat16)
+    for h in range(chunks):
+        q_own[h] = q_t[:, h * CHUNK : (h + 1) * CHUNK].astype(jnp.bfloat16)
 
     def q_copy(d, h, k):
         src = q_own.at[h] if isinstance(k, int) and k == 0 else q_buf.at[d, k - 1, h]
@@ -307,7 +307,7 @@
 
     for d in range(2):
         f_copy(d, 0).start()
-        for h in (d, 1 - d):
+        for h in range(chunks):
             q_copy(d, h, 0).start()
 
     def unit_columns(v):
@@ -322,7 +322,7 @@
     k_unit_t = jnp.transpose(k_unit)
     gates = jnp.transpose(mm(normed[...], w_parts[3]))
     values_t[...] = v_t.astype(jnp.bfloat16)
-    units = unit_columns(jnp.concatenate([q_own[0], q_own[1]], axis=1).astype(jnp.float32))
+    units = unit_columns(q_t.astype(jnp.bfloat16).astype(jnp.float32))
     for b in range(prefill // BLK):
         key_unit[b] = k_unit[b * BLK : (b + 1) * BLK, :]
     for p in range(prefill // (2 * BLK)):
@@ -348,29 +348,28 @@
             kv_copy(d, k, j).wait_recv()
         return pick([kv_buf[d, k - 1, s] for s in range(NX)])
 
-    far_sides = tuple(tuple(range(d * NX // 2, (d + 1) * NX // 2)) for d in range(2))
     far_rows = (beyond + 1) * plane - plane // 2
 
-    def split_far(d):
-        for k in range(reach, depth + 1):
-            if k == reach:
-                keys, vals = split_near(d, k)
-            elif k < depth:
-                for j in range(NX):
-                    kv_copy(d, k, j).wait_recv()
-                keys, vals = pick([kv_buf[d, k - 1, s] for s in range(NX)])
-            else:
-                for s in far_sides[d]:
-                    kv_copy(d, k, lax.rem(x + NX - s, NX)).wait_recv()
-                keys, vals = pick([kv_buf[d, k - 1, s] for s in far_sides[d]])
-            at = (k - reach) * plane
-            keys_far[d, at : at + keys.shape[0], :] = keys
-            values_far[d, :, at : at + keys.shape[0]] = vals
-
-    def bias_of(fill_row, server, first, count):
+    def split_far(d, k):
+        if k == reach:
+            keys, vals = split_near(d, k)
+        elif k < depth:
+            for j in range(NX):
+                kv_copy(d, k, j).wait_recv()
+            keys, vals = pick([kv_buf[d, k - 1, s] for s in range(NX)])
+        else:
+            for j in range(d, NX, 2):
+                kv_copy(d, k, j).wait_recv()
+            first = lax.rem(x + d, 2)
+            keys, vals = pick([kv_buf[d, k - 1, first + s] for s in range(0, NX, 2)])
+        at = (k - reach) * plane
+        keys_far[d, at : at + keys.shape[0], :] = keys
+        values_far[d, :, at : at + keys.shape[0]] = vals
+
+    def bias_of(fill_row, base, count, skip=0):
         row_id = lax.broadcasted_iota(jnp.int32, (count, 128), 0)
         lane_id = lax.broadcasted_iota(jnp.int32, (count, 128), 1)
-        slot_mine = lane_id == server * (NX * 2) + first + row_id // PAGE
+        slot_mine = lane_id == base + row_id // PAGE + skip * (row_id // (2 * PAGE))
         fills = jnp.sum(jnp.where(slot_mine, fill_row, 0.0), axis=1, keepdims=True)
         in_page = lax.rem(row_id[:, 0:1], PAGE).astype(jnp.float32)
         return jnp.where(in_page < fills, 0.0, NEG)
@@ -379,17 +378,17 @@
         top, total, grown = soften(mm(keys, q) * scale + bias)
         return top, total, mm(vals, grown)
 
-    def keep_part(d, k, h, result):
-        top, total, acc = result
-        part_acc[d, k - 1, h] = acc
-        part_ml[d, k - 1, h, 0:1, :] = top
-        part_ml[d, k - 1, h, 1:2, :] = total
-
     def absorb(d, k):
         keys, vals = split_near(d, k)
-        bias = bias_of(fill_buf[d, k - 1][0:1, :], z, 0, plane)
-        for h in range(2):
-            keep_part(d, k, h, attend(keys, vals, bias, q_buf[d, k - 1, h]))
+        bias = bias_of(fill_buf[d, k - 1][0:1, :], z * (NX * 2), plane)
+        for h in range(0, chunks, 2):
+            q = jnp.concatenate([q_buf[d, k - 1, h], q_buf[d, k - 1, h + 1]], axis=1)
+            top, total, acc = attend(keys, vals, bias, q)
+            for u in range(2):
+                columns = slice(u * CHUNK, (u + 1) * CHUNK)
+                part_acc[d, k - 1, h + u] = acc[:, columns]
+                part_ml[d, k - 1, h + u, 0:1, :] = top[:, columns]
+                part_ml[d, k - 1, h + u, 1:2, :] = total[:, columns]
 
     def memory_pair(p):
         reads = []
@@ -411,16 +410,16 @@
         for j in range(1, NX):
             home_copy(j).wait_recv()
         keys0, vals0 = pick([kv_home[s] for s in range(NX)])
-        bias0 = bias_of(fill_own[0:1, :], z, 0, plane)
+        bias0 = bias_of(fill_own[0:1, :], z * (NX * 2), plane)
         persist_t = jnp.transpose(persist_ref[1].astype(jnp.float32)).astype(jnp.bfloat16)
-        for h in range(2):
-            count = (h + 1) * half
+        for h in range(chunks):
+            count = (h + 1) * CHUNK
             q = q_own[h]
             s_c = mm(keys0, q) * scale + bias0
             s_p = mm(persist_ref[0], q) * scale
             s_t = mm(keys_own[0:count, :], q) * scale
-            order = lax.broadcasted_iota(jnp.int32, (count, half), 0)
-            place = lax.broadcasted_iota(jnp.int32, (count, half), 1) + h * half
+            order = lax.broadcasted_iota(jnp.int32, (count, CHUNK), 0)
+            place = lax.broadcasted_iota(jnp.int32, (count, CHUNK), 1) + h * CHUNK
             s_t = jnp.where(order <= place, s_t, NEG)
             top_c, total_c, grown_c = soften(s_c)
             top_t, total_t, grown_t = soften(s_t)
@@ -432,26 +431,23 @@
             home_ml[h, 0:1, :] = top
             home_ml[h, 1:2, :] = total_c * e_c + total_t * e_t + total_p * e_p
 
-    order_of = lambda d: (d, 1 - d)
-
     def gather_step(k):
         for d in range(2):
             f_done(d, k - 1).wait_recv()
             f_copy(d, k).start()
-            for h in order_of(d):
+            for h in range(chunks):
                 q_done(d, h, k - 1).wait_recv()
                 q_copy(d, h, k).start()
 
-    for d in range(2):
-        split_far(d)
-
-    def gather_loop(k, carry):
+    far_ks = list(range(depth, reach, -1))
+    for k in range(1, reach):
         gather_step(k)
         for d in range(2):
             absorb(d, k)
-        return carry
-
-    lax.fori_loop(1, reach, gather_loop, 0)
+        if k > 1:
+            for far_k in far_ks[k - 2 : k - 1] if k < reach - 1 else far_ks[k - 2 :]:
+                for d in range(2):
+                    split_far(d, far_k)
     spread_mid(wout)
 
     def ring_copies(d, h, k):
@@ -500,6 +496,8 @@
         ring_send(d, h, k, *join(partial(d, h, k), received(d, h, k + 1)))
 
     last = reach - 1
+    for d in range(2):
+        split_far(d, reach)
     biases = []
     for d in range(2):
         f_done(d, last).wait_recv()
@@ -507,12 +505,14 @@
         pieces = []
         for hop in range(beyond + 1):
             server = lax.rem(z + nz + (1 - 2 * d) * hop, nz)
-            first, count = (d * NX, plane // 2) if hop == beyond else (0, plane)
-            pieces.append(bias_of(fill_row, server, first, count))
+            if hop < beyond:
+                pieces.append(bias_of(fill_row, server * (NX * 2), plane))
+            else:
+                base = server * (NX * 2) + 2 * lax.rem(x + d, 2)
+                pieces.append(bias_of(fill_row, base, plane // 2, 2))
         biases.append(jnp.concatenate(pieces, axis=0))
-    for i in range(2):
+    for h in range(chunks):
         for d in range(2):
-            h = order_of(d)[i]
             q_done(d, h, last).wait_recv()
             top, total, acc = attend(
                 keys_far[d], values_far[d], biases[d], q_buf[d, last, h]
@@ -524,9 +524,9 @@
     pairs = prefill // (2 * BLK)
 
     def ring_loop(i, carry):
-        for n in range(2):
+        for h in range(chunks):
             for d in range(2):
-                ring_join(d, order_of(d)[n], last - i)
+                ring_join(d, h, last - i)
         pl.when(i <= pairs)(lambda: memory_pair(i - 1))
         return carry
 
@@ -542,16 +542,14 @@
     def head_arrival(g):
         return remote(hout_buf.at[g], hrecv.at[g], h_send.at[g], h_recv.at[g], (req, g))
 
-    per = heads // 2
-    for h in range(2):
+    per = heads // chunks
+    for h in range(chunks):
         mine = home_acc[h], home_ml[h, 0:1, :], home_ml[h, 1:2, :]
-        for d in (h, 1 - h):
+        for d in range(2):
             mine = join(mine, received(d, h, 0))
         attended = mine[0] / mine[2]
         mean = jnp.mean(attended * attended, axis=0, keepdims=True)
-        some = pairs // 2
-        extra = jnp.concatenate([extra_t[h * some + p] for p in range(some)], axis=1)
-        out = attended * lax.rsqrt(mean + UNIT_EPS) + extra
+        out = attended * lax.rsqrt(mean + UNIT_EPS) + extra_t[h]
         turned = jnp.transpose(out).astype(jnp.bfloat16)
         for g in range(h * per, (h + 1) * per):
             hout_buf[g] = turned[(g - h * per) * rows : (g - h * per + 1) * rows, :]
@@ -580,12 +578,12 @@
         for k in range(reach + 1, depth):
             for d in range(2):
                 kv_copy(d, k, j).wait_send()
-        kv_copy(side, depth, j).wait_send()
+        kv_copy(j % 2, depth, j).wait_send()
 
     def ends(k, carry):
         for d in range(2):
             f_done(d, k).wait_send()
-            for h in range(2):
+            for h in range(chunks):
                 q_done(d, h, k).wait_send()
                 for c in ring_copies(d, h, k):
                     c.wait_send()
@@ -622,7 +620,8 @@
     depth = nz // 2
     rows, width = tokens.shape[1], tokens.shape[2]
     prefill = rows * heads
-    half = prefill // 2
+    chunks = prefill // CHUNK
+    half = CHUNK
     blocks = prefill // BLK
     span = cache_page_slots.shape[2] * 2
     bf, f32 = jnp.bfloat16, jnp.float32
@@ -632,7 +631,7 @@
     sems = pltpu.SemaphoreType.DMA
     reach = min(REACH, depth - 1)
     pairs = blocks // 2
-    rings = (2, reach, 2)
+    rings = (2, reach, chunks)
     far_rows = (depth - reach + 1) * NX * span // 2 - NX * span // 4
     scratch = [
         pltpu.VMEM((heads, rows, width), bf),
@@ -642,7 +641,7 @@
         pltpu.VMEM((prefill, width), bf),
         pltpu.VMEM((NX, span, HD), bf),
         pltpu.VMEM((2, depth, NX, span, HD), bf),
-        pltpu.VMEM((2, HD, half), bf),
+        pltpu.VMEM((chunks, HD, half), bf),
         pltpu.VMEM(rings + (HD, half), bf),
         pltpu.VMEM((8, 128), f32),
         pltpu.VMEM((2, reach, 8, 128), f32),
@@ -665,8 +664,8 @@
         pltpu.VMEM(rings + (2, half), f32),
         pltpu.VMEM(rings + (HD, half), bf),
         pltpu.VMEM(rings + (2, half), f32),
-        pltpu.VMEM((2, HD, half), f32),
-        pltpu.VMEM((2, 2, half), f32),
+        pltpu.VMEM((chunks, HD, half), f32),
+        pltpu.VMEM((chunks, 2, half), f32),
         pltpu.VMEM((heads, rows, HD), bf),
         pltpu.VMEM((heads, rows, HD), bf),
         sems((11,)),
@@ -679,14 +678,14 @@
         sems((2, depth, NX)),
         sems((2, depth, NX)),
         sems((2, depth)),
-        sems((2, 2, reach)),
-        sems((2, 2, reach)),
+        sems((2, chunks, reach)),
+        sems((2, chunks, reach)),
         sems((2, reach)),
         sems((2, reach)),
-        sems((2, 2, reach)),
-        sems((2, 2, reach)),
-        sems((2, 2, reach)),
-        sems((2, 2, reach)),
+        sems((2, chunks, reach)),
+        sems((2, chunks, reach)),
+        sems((2, chunks, reach)),
+        sems((2, chunks, reach)),
         sems((heads,)),
         sems((heads,)),
     ]

time: 97.3 us -> 85.8 us (0.88)
  Pallas kernels: 93.9 us -> 82.3 us
    pallas_call x1, Pallas kernels: 92.2 us -> 80.7 us  [shards(): pl.pallas_call(functools.partial(kernel, nz, ny), out_shape=(jax.ShapeDty...]
where the time goes in v3:
time: 85.8 us; the launch traced here: 85.6 us
  Pallas kernels  82.3 us (96%)
  between operations  3.22 us (4%)
    pallas_call x1, Pallas kernels, shards(): pl.pallas_call(functools.partial(kernel, nz, ny), out_shape=(jax.ShapeDty...  80.7 us

profile of v3, /device:TPU:1, one launch (start us, length us, event | category | flops | bytes accessed | tf_op | source)
XLA Modules:
  0.0 85.6 jit_solution(8747224792695591016)
XLA Ops:
  3.2 80.7 %shard_map.149 = (bf16[64,1024]{1,0:T(8,128)(2,1)}, f32[2,128,128]{2,1,0:T(8,128)}) custom-call(bf16[64,1024]{1,0:T(8,128)(2,1)} %bitcast.11, bf16[8,128]{1,0:T(8,128)(2,1)} %bitcast.13, bf16[4096,128]{1,0:T(8,128)(2,1)} %bitcast.10, bf16[128,1024]{1,0:T(8,128)(2,1)} %out_weight_ref.1, bf16[2,16,128]{2,1,0:T(8,128)(2,1)} %persist_ref.1, ...), custom_call_target="tpu_custom_call" | custom-call | tf_op jit(solution)/shard_map/pallas_call | solution.py:692
  83.9 1.7 %shard_map.150 = (bf16[64,1024]{1,0:T(8,128)(2,1)}, f32[2,128,128]{2,1,0:T(8,128)}) custom-call(bf16[64,1024]{1,0:T(8,128)(2,1)} %get-tuple-element.6.layer_ref, f32[2,128,128]{2,1,0:T(8,128)} %get-tuple-element.7.state_ref), custom_call_target="tpu_custom_call" | custom-call | tf_op jit(solution)/shard_map/pallas_call | solution.py:720

commit v4 on v3

--- a/solution.py
+++ b/solution.py
@@ -241,13 +241,14 @@
 
     spread_mid(tok)
     for k in range(1, reach + 1):
+        if k == reach - 1:
+            home_stay().start()
+            for j in range(1, NX):
+                home_copy(j).start()
         for d in range(2):
             kv_stay(d, k).start()
             for j in range(1, NX):
                 kv_copy(d, k, j).start()
-    home_stay().start()
-    for j in range(1, NX):
-        home_copy(j).start()
 
     ids = lax.broadcasted_iota(jnp.int32, (1, 128), 1)
     filled = jnp.clip(length_ref[0] - ids * PAGE, 0, PAGE).astype(jnp.float32)
@@ -448,6 +449,8 @@
             for far_k in far_ks[k - 2 : k - 1] if k < reach - 1 else far_ks[k - 2 :]:
                 for d in range(2):
                     split_far(d, far_k)
+        if k == reach - 2:
+            own_attention()
     spread_mid(wout)
 
     def ring_copies(d, h, k):
@@ -519,7 +522,6 @@
             )
             ring_send(d, h, last, acc, top, total)
 
-    own_attention()
     spread_late(wout)
     pairs = prefill // (2 * BLK)
 

time: 85.8 us -> 86.9 us (1.013)
  Pallas kernels: 82.3 us -> 83.5 us
    pallas_call x1, Pallas kernels: 80.7 us -> 81.8 us  [shards(): pl.pallas_call(functools.partial(kernel, nz, ny), out_shape=(jax.ShapeDty...]
where the time goes in v4:
time: 86.9 us; the launch traced here: 86.7 us
  Pallas kernels  83.5 us (96%)
  between operations  3.22 us (4%)
    pallas_call x1, Pallas kernels, shards(): pl.pallas_call(functools.partial(kernel, nz, ny), out_shape=(jax.ShapeDty...  81.8 us

profile of v4, /device:TPU:1, one launch (start us, length us, event | category | flops | bytes accessed | tf_op | source)
XLA Modules:
  0.0 86.7 jit_solution(6495155689864790528)
XLA Ops:
  3.2 81.8 %shard_map.149 = (bf16[64,1024]{1,0:T(8,128)(2,1)}, f32[2,128,128]{2,1,0:T(8,128)}) custom-call(bf16[64,1024]{1,0:T(8,128)(2,1)} %bitcast.11, bf16[8,128]{1,0:T(8,128)(2,1)} %bitcast.13, bf16[4096,128]{1,0:T(8,128)(2,1)} %bitcast.10, bf16[128,1024]{1,0:T(8,128)(2,1)} %out_weight_ref.1, bf16[2,16,128]{2,1,0:T(8,128)(2,1)} %persist_ref.1, ...), custom_call_target="tpu_custom_call" | custom-call | tf_op jit(solution)/shard_map/pallas_call | solution.py:694
  85.0 1.7 %shard_map.150 = (bf16[64,1024]{1,0:T(8,128)(2,1)}, f32[2,128,128]{2,1,0:T(8,128)}) custom-call(bf16[64,1024]{1,0:T(8,128)(2,1)} %get-tuple-element.6.layer_ref, f32[2,128,128]{2,1,0:T(8,128)} %get-tuple-element.7.state_ref), custom_call_target="tpu_custom_call" | custom-call | tf_op jit(solution)/shard_map/pallas_call | solution.py:722
